TPU v7x, 128 devices: a whole 4x4x4 slice. The times are simulated.
128 devices in a mesh: dp: 32 (over y, z, core), bn: 4 (over x).
Axes of the slice: x: 4, y: 4, z: 4, core: 2. Of those that a mesh axis runs over, the one named last changes fastest.
Arguments:
- key_feats: bfloat16 [1024, 12, 16, 2048], P(('dp', 'bn')), may hold values from -22 to 22
- clip_starts: int32 [1024], P(('dp', 'bn')), may hold values from 0 to 4
- shuffle: int32 [4, 32], P('bn'), may hold values from 0 to 31, each once within a row
- query_feats: bfloat16 [1024, 2048], P(('dp', 'bn')), may hold values from -6 to 6
- conv_time: bfloat16 [3, 2048, 512], replicated, may hold values from -0.078125 to 0.078125
- conv_space: bfloat16 [9, 512, 512], replicated, may hold values from -0.09375 to 0.09375
- conv_expand: bfloat16 [512, 2048], replicated, may hold values from -0.25 to 0.25
- gain_one: float32 [512], replicated, may hold values from 0.25 to 1.75
- shift_one: float32 [512], replicated, may hold values from -3 to 3
- gain_two: float32 [512], replicated, may hold values from 0.25 to 1.75
- shift_two: float32 [512], replicated, may hold values from -3 to 3
- gain_three: float32 [2048], replicated, may hold values from 0.25 to 1.75
- shift_three: float32 [2048], replicated, may hold values from -3 to 3
- w_key: bfloat16 [2048, 128], replicated, may hold values from -0.125 to 0.125
- w_query: bfloat16 [2048, 128], replicated, may hold values from -0.125 to 0.125
- queue: bfloat16 [16384, 128], replicated, may hold values from -6 to 6
Outputs:
- keys: bfloat16 [1024, 128], P(('dp', 'bn'))
- query_grad: float32 [2048, 128], replicated
Inputs may be any that keep to these rules, and one draw needn't show every extreme that they name: `shuffle`: each row is a permutation of 0 to 31.
All inputs are finite; a program needn't handle non-finite values.
Results may differ from a plain program's by a relative error of at most 0.0061.
Values may be sent and summed in bfloat16 or wider, within the bound.
A program may use at most 128 MiB of HBM per device.

v0:
```python
import jax
import jax.numpy as jnp
from jax import lax
from jax.sharding import PartitionSpec as P

FRAMES = 8
SIDE = 4


SHARPNESS_DIVISOR = 0.2
EPSILON = 1e-05


def pick_frames(features, starts):

    def single(clip_feats, first_frame):
        return lax.dynamic_slice_in_dim(clip_feats, first_frame, FRAMES, 0)

    return jax.vmap(single)(features, starts)


def time_conv(values, weights):
    padded = jnp.pad(values, ((0, 0), (1, 1), (0, 0), (0, 0)))
    length = values.shape[1]
    summed = jnp.zeros(values.shape[:3] + (weights.shape[2],), jnp.float32)
    for offset in range(3):
        summed = summed + jnp.einsum(
            "afsc,cd->afsd",
            padded[:, offset : offset + length],
            weights[offset],
            preferred_element_type=jnp.float32,
        )
    return summed


def space_conv(values, weights):
    square_grid = values.reshape(values.shape[0], values.shape[1], SIDE, SIDE, values.shape[3])
    padded = jnp.pad(square_grid, ((0, 0), (0, 0), (1, 1), (1, 1), (0, 0)))
    summed = jnp.zeros(
        (values.shape[0], values.shape[1], SIDE, SIDE, weights.shape[2]), jnp.float32
    )
    for row_shift in range(3):
        for col_shift in range(3):
            window = padded[:, :, row_shift : row_shift + SIDE, col_shift : col_shift + SIDE]
            summed = summed + jnp.einsum(
                "afhwc,cd->afhwd",
                window,
                weights[3 * row_shift + col_shift],
                preferred_element_type=jnp.float32,
            )
    return summed.reshape(values.shape[0], values.shape[1], SIDE * SIDE, weights.shape[2])


def batch_norm(values, total_sum, squares, row_count, gain_row, shift_row):
    center = total_sum / row_count
    spread = squares / row_count - center * center
    return (values - center) * (gain_row * lax.rsqrt(spread + EPSILON)) + shift_row


def encode(values, params, moments, row_count):
    (
        conv_time,
        conv_space,
        conv_expand,
        gain_one,
        shift_one,
        gain_two,
        shift_two,
        gain_three,
        shift_three,
        w_key,
    ) = params
    first_out = time_conv(values, conv_time)
    total_sum, squares = moments(first_out)
    act_one = jnp.maximum(
        batch_norm(first_out, total_sum, squares, row_count, gain_one, shift_one), 0.0
    ).astype(jnp.bfloat16)
    second = space_conv(act_one, conv_space)
    total_sum, squares = moments(second)
    act_two = jnp.maximum(
        batch_norm(second, total_sum, squares, row_count, gain_two, shift_two), 0.0
    ).astype(jnp.bfloat16)
    third_out = jnp.einsum(
        "afsc,cd->afsd", act_two, conv_expand, preferred_element_type=jnp.float32
    )
    total_sum, squares = moments(third_out)
    merged = jnp.maximum(
        batch_norm(third_out, total_sum, squares, row_count, gain_three, shift_three)
        + values.astype(jnp.float32),
        0.0,
    )
    pooled = jnp.mean(merged, axis=(1, 2)).astype(jnp.bfloat16)
    projected = jnp.dot(pooled, w_key, preferred_element_type=jnp.float32)
    return (
        projected * lax.rsqrt(jnp.sum(projected * projected, axis=-1, keepdims=True) + 1e-06)
    ).astype(jnp.bfloat16)


def query_terms(query_feats, own_keys, w_query, queue):
    projected = jnp.dot(query_feats, w_query, preferred_element_type=jnp.float32)
    length = jnp.sqrt(jnp.sum(projected * projected, axis=-1, keepdims=True) + 1e-06)
    anchor_direction = projected / length
    queue_wide = queue.astype(jnp.float32)
    memory_bank_directions = (
        queue_wide * lax.rsqrt(jnp.sum(queue_wide * queue_wide, axis=-1, keepdims=True) + 1e-06)
    ).astype(jnp.bfloat16)
    collected_encodings = own_keys.astype(jnp.float32)
    matching_scores = jnp.sum(anchor_direction * collected_encodings, axis=-1) / SHARPNESS_DIVISOR
    distractor_scores = (
        jnp.einsum(
            "nf,ef->ne",
            anchor_direction.astype(jnp.bfloat16),
            memory_bank_directions,
            preferred_element_type=jnp.float32,
        )
        / SHARPNESS_DIVISOR
    )
    partition = jnp.exp(matching_scores) + jnp.sum(jnp.exp(distractor_scores), axis=-1)
    log_total = jnp.log(partition)
    weight_pos = jnp.exp(matching_scores - log_total)
    weight_neg = jnp.exp(distractor_scores - log_total[:, None]).astype(jnp.bfloat16)
    retrieved_samples = (
        jnp.dot(weight_neg, memory_bank_directions, preferred_element_type=jnp.float32)
        + (weight_pos - 1.0)[:, None] * collected_encodings
    )
    anchor_loss_derivative = retrieved_samples / SHARPNESS_DIVISOR
    radial = jnp.sum(anchor_direction * anchor_loss_derivative, axis=-1, keepdims=True)
    return ((anchor_loss_derivative - radial * anchor_direction) / length).astype(jnp.bfloat16)


def local(
    key_feats,
    clip_starts,
    shuffle,
    query_feats,
    conv_time,
    conv_space,
    conv_expand,
    gain_one,
    shift_one,
    gain_two,
    shift_two,
    gain_three,
    shift_three,
    w_key,
    w_query,
    queue,
):
    params = (
        conv_time,
        conv_space,
        conv_expand,
        gain_one,
        shift_one,
        gain_two,
        shift_two,
        gain_three,
        shift_three,
        w_key,
    )
    chosen = pick_frames(key_feats, clip_starts)
    peer_count = lax.axis_size("dp")
    groups = lax.axis_size("bn")
    target = shuffle[0, lax.axis_index("dp")]
    row_count = groups * chosen.shape[0] * chosen.shape[1] * chosen.shape[2]
    positions = jnp.arange(peer_count, dtype=jnp.int32)
    matches = (shuffle[0][:, None] == positions[None, :]).astype(jnp.int32)
    inverse = jnp.sum(positions[:, None] * matches, axis=0)
    pieces = chosen.reshape((peer_count, -1, chosen.shape[3]))
    relayed = lax.all_to_all(pieces, "dp", split_axis=0, concat_axis=0, tiled=True)
    resent = jnp.take(relayed, inverse, axis=0)
    arrived = lax.all_to_all(resent, "dp", split_axis=0, concat_axis=0, tiled=True)
    hosted = arrived.reshape(chosen.shape)

    def group_moments(values):
        return lax.psum(
            (jnp.sum(values, axis=(0, 1, 2)), jnp.sum(values * values, axis=(0, 1, 2))), "bn"
        )

    encoded = encode(hosted, params, group_moments, row_count)
    key_table = lax.all_gather(encoded, "dp", axis=0, tiled=True)
    own_keys = lax.dynamic_slice_in_dim(key_table, target * encoded.shape[0], encoded.shape[0], 0)
    grad_proj = query_terms(query_feats, own_keys, w_query, queue)
    grad_part = jnp.einsum("nc,ne->ce", query_feats, grad_proj, preferred_element_type=jnp.float32)
    query_grad = lax.psum(grad_part, ("dp", "bn"))
    return (own_keys, query_grad)


def solution(mesh):
    placed = (
        P(("dp", "bn"), None, None, None),
        P(("dp", "bn")),
        P("bn", None),
        P(("dp", "bn"), None),
        P(),
        P(),
        P(),
        P(),
        P(),
        P(),
        P(),
        P(),
        P(),
        P(),
        P(),
        P(),
    )
    return jax.shard_map(
        local, mesh=mesh, in_specs=placed, out_specs=(P(("dp", "bn"), None), P()), check_vma=False
    )
```

profile of v0, /device:TPU:1, one launch (start us, length us, event | category | flops | bytes accessed | tf_op | source)
XLA Modules:
  0.0 413.6 jit_solution(8654129349568916141)
XLA Ops:
  7.2 0.0 copy-start
  7.2 0.0 copy-start.13
  7.2 6.7 %copy.23 = bf16[8,12,16,2048]{3,2,0,1:T(8,128)(2,1)} copy(bf16[8,12,16,2048]{3,2,1,0:T(8,128)(2,1)} %param.16) | data formatting | bytes 12582912 | tf_op args[0]
  13.9 0.0 copy-done.13
  13.9 5.6 %gather_fusion.1 = bf16[8,8,16,2048]{3,2,1,0:T(8,128)(2,1)} fusion(bf16[8,12,16,2048]{3,2,0,1:T(8,128)(2,1)} %copy.23, s32[8]{0:T(128)S(1)} %fusion.71), kind=kCustom, calls=%fused_computation.1 | custom fusion | bytes 8388736 | tf_op jit(solution)/shard_map/vmap()/gather | solution.py:17
  19.6 9.8 %all-to-all-start = ((bf16[32,32,2048]{2,1,0:T(8,128)(2,1)}), bf16[32,32,2048]{2,1,0:T(8,128)(2,1)}, u32[]{:S(2)}, u32[]{:S(2)}) async-start(bf16[32,32,2048]{2,1,0:T(8,128)(2,1)} %bitcast.142), calls=%async_computation | async-start | bytes 8388608 | tf_op jit(solution)/shard_map/all_to_all | solution.py:170
  29.4 0.0 copy-done.14
  29.4 0.1 select_reduce_fusion
  29.5 52.0 %all-to-all-done = bf16[32,32,2048]{2,1,0:T(8,128)(2,1)} async-done(((bf16[32,32,2048]{2,1,0:T(8,128)(2,1)}), bf16[32,32,2048]{2,1,0:T(8,128)(2,1)}, u32[]{:S(2)}, u32[]{:S(2)}) %all-to-all-start) | async-done | bytes 4194336 | tf_op jit(solution)/shard_map/all_to_all | solution.py:170
  81.5 5.0 %gather_fusion = bf16[32,32,2048]{2,1,0:T(8,128)(2,1)} fusion(bf16[32,32,2048]{2,1,0:T(8,128)(2,1)} %all-to-all-done, s32[1024]{0:T(1024)S(1)} %pad_clamp_fusion), kind=kCustom, calls=%fused_computation | custom fusion | bytes 8388736 | tf_op jit(solution)/shard_map/jit(_take)/gather | solution.py:171
  86.4 4.6 %broadcast_select_fusion = bf16[32,32,2048]{2,1,0:T(8,128)(2,1)} fusion(bf16[32,32,2048]{2,1,0:T(8,128)(2,1)} %gather_fusion, pred[32]{0:T(512)(128)(4,1)S(1)} %compare_and_fusion), kind=kLoop, calls=%fused_computation.9 | loop fusion | flops 2097152 | bytes 8388640 | tf_op jit(solution)/shard_map/jit(_take)/select_n | solution.py:171
  91.1 7.2 %all-to-all-start.1 = ((bf16[32,32,2048]{2,1,0:T(8,128)(2,1)}), bf16[32,32,2048]{2,1,0:T(8,128)(2,1)}, u32[]{:S(2)}, u32[]{:S(2)}) async-start(bf16[32,32,2048]{2,1,0:T(8,128)(2,1)} %broadcast_select_fusion), calls=%async_computation.1 | async-start | bytes 8388608 | tf_op jit(solution)/shard_map/all_to_all | solution.py:172
  98.3 0.0 all-reduce.8.cloned.1.call-start
  98.3 0.6 fusion.77
  100.9 0.0 copy-done.3
  100.9 0.0 copy-done.5
  100.9 0.0 copy-start.1
  100.9 0.3 multiply_reduce_fusion.4
  101.2 4.2 %fusion = f32[16384]{0:T(1024)S(1)} fusion(bf16[16384,128]{1,0:T(8,128)(2,1)} %param.31), kind=kLoop, calls=%fused_computation.5 | loop fusion | flops 6275072 | bytes 4259840 | tf_op jit(solution)/shard_map/reduce_sum | solution.py:105
  105.5 0.0 copy-done.1
  105.5 2.5 exponential_reduce_fusion
  107.9 42.5 %all-to-all-done.1 = bf16[32,32,2048]{2,1,0:T(8,128)(2,1)} async-done(((bf16[32,32,2048]{2,1,0:T(8,128)(2,1)}), bf16[32,32,2048]{2,1,0:T(8,128)(2,1)}, u32[]{:S(2)}, u32[]{:S(2)}) %all-to-all-start.1) | async-done | bytes 4194336 | tf_op jit(solution)/shard_map/all_to_all | solution.py:172
  150.4 5.2 %fusion.6 = f32[8,8,16,512]{3,2,1,0:T(8,128)S(1)} fusion(bf16[8,8,16,2048]{3,2,1,0:T(8,128)(2,1)} %bitcast.6, bf16[3,2048,512]{2,1,0:T(8,128)(2,1)} %param.20), kind=kOutput, calls=%fused_computation.15 | convolution fusion | flops 2147483648 | bytes 8388608 | tf_op jit(solution)/shard_map/afsc,cd->afsd/dot_general | solution.py:27
  155.6 5.0 %fusion.8 = f32[8,8,16,512]{3,2,1,0:T(8,128)S(1)} fusion(bf16[8,8,16,2048]{3,2,1,0:T(8,128)(2,1)} %bitcast.6, bf16[3,2048,512]{2,1,0:T(8,128)(2,1)} %param.20), kind=kOutput, calls=%fused_computation.17 | convolution fusion | flops 1879048192 | bytes 8388608 | tf_op jit(solution)/shard_map/afsc,cd->afsd/dot_general | solution.py:27
  160.6 0.0 copy-start.8
  160.6 0.0 copy-start.11
  160.7 6.6 %fusion.76 = (f32[512]{0:T(512)S(1)}, f32[512]{0:T(512)S(1)}, f32[8,8,16,512]{3,2,1,0:T(8,128)}) fusion(bf16[8,8,16,2048]{3,2,1,0:T(8,128)(2,1)} %bitcast.6, bf16[3,2048,512]{2,1,0:T(8,128)(2,1)} %param.20, f32[8,8,16,512]{3,2,1,0:T(8,128)S(1)} %fusion.8, f32[8,8,16,512]{3,2,1,0:T(8,128)S(1)} %fusion.6), kind=kOutput, calls=%fused_computation.113 | convolution fusion | flops 1881668608 | bytes 12587008 | tf_op jit(solution)/shard_map/afsc,cd->afsd/dot_general | solution.py:27
  167.2 8.6 %all-reduce.5 = (f32[512]{0:T(512)S(1)}, f32[512]{0:T(512)S(1)}) all-reduce(f32[512]{0:T(512)S(1)} %get-tuple-element.11, f32[512]{0:T(512)S(1)} %get-tuple-element.10), channel_id=1, replica_groups=mesh['dp'=32,'bn'=4] {'bn'}, use_global_device_ids=true, to_apply=%region_4.5 | all-reduce | flops 1024 | bytes 8192 | tf_op jit(solution)/shard_map/psum | solution.py:176
  175.8 0.0 copy-done.8
  175.9 0.0 slice-start
  175.9 2.1 maximum_convert_fusion
  178.0 0.6 copy.42
  178.6 0.0 slice-start.1
  178.6 1.8 fusion.34
  180.4 1.7 fusion.36
  182.2 1.7 fusion.38
  184.0 0.7 fusion.40
  184.7 0.7 fusion.42
  185.4 0.7 fusion.44
  186.1 0.7 fusion.46
  186.8 0.7 fusion.48
  187.5 0.0 copy-start.9
  187.5 0.0 copy-start.12
  187.5 2.6 fusion.75
  190.2 6.0 %all-reduce.4 = (f32[512]{0:T(512)S(1)}, f32[512]{0:T(512)S(1)}) all-reduce(f32[512]{0:T(512)S(1)} %get-tuple-element.9, f32[512]{0:T(512)S(1)} %get-tuple-element.8), channel_id=1, replica_groups=mesh['dp'=32,'bn'=4] {'bn'}, use_global_device_ids=true, to_apply=%region_8.9 | all-reduce | flops 1024 | bytes 8192 | tf_op jit(solution)/shard_map/psum | solution.py:176
  196.2 0.0 copy-done
  196.2 0.0 copy-done.12
  196.2 0.0 copy-start.6
  196.2 0.0 copy-start.7
  196.2 8.0 %fusion.74 = (f32[2048]{0:T(1024)S(1)}, f32[2048]{0:T(1024)S(1)}, f32[8,8,16,2048]{3,2,1,0:T(8,128)}) fusion(bf16[512,2048]{1,0:T(8,128)(2,1)S(1)} %copy-done, f32[8,8,16,512]{3,1,2,0:T(8,128)} %bitcast.145, f32[512]{0:T(512)S(1)} %copy-done.12, f32[512]{0:T(512)S(1)} %get-tuple-element.23, f32[512]{0:T(512)S(1)} %get-tuple-element.22), kind=kOutput, calls=%fused_computation.111 | convolution fusion | flops 2156392448 | bytes 12605440 | tf_op jit(solution)/shard_map/afsc,cd->afsd/dot_general | solution.py:83
  204.2 12.4 %all-reduce.3 = (f32[2048]{0:T(1024)S(1)}, f32[2048]{0:T(1024)S(1)}) all-reduce(f32[2048]{0:T(1024)S(1)} %get-tuple-element.7, f32[2048]{0:T(1024)S(1)} %get-tuple-element.6), channel_id=1, replica_groups=mesh['dp'=32,'bn'=4] {'bn'}, use_global_device_ids=true, to_apply=%region_12.13 | all-reduce | flops 4096 | bytes 32768 | tf_op jit(solution)/shard_map/psum | solution.py:176
  216.6 0.0 copy-start.4
  216.6 0.0 copy-start.2
  216.6 5.8 %maximum_reduce_fusion = f32[8,2048]{1,0:T(8,128)S(1)} fusion(bf16[8,8,16,2048]{3,2,1,0:T(8,128)(2,1)} %bitcast.6, f32[8,8,16,2048]{3,2,1,0:T(8,128)} %get-tuple-element.32, f32[2048]{0:T(1024)S(1)} %copy-done.7, f32[2048]{0:T(1024)S(1)} %get-tuple-element.21, f32[2048]{0:T(1024)S(1)} %get-tuple-element.20), kind=kLoop, calls=%fused_computation.7 | loop fusion | flops 14663680 | bytes 12673024 | tf_op jit(solution)/shard_map/reduce_sum | solution.py:92
  222.5 0.3 multiply_reduce_fusion.5
  222.8 0.1 multiply_convert_fusion.2
  222.8 32.2 %all_gather.3 = bf16[256,128]{1,0:T(8,128)(2,1)S(1)} all-gather(bf16[8,128]{1,0:T(8,128)(2,1)S(1)} %multiply_convert_fusion.2), channel_id=1, replica_groups=mesh['dp'=32,'bn'=4] {'dp'}, dimensions={0}, use_global_device_ids=true | all-gather | bytes 67584 | tf_op jit(solution)/shard_map/all_gather | solution.py:181
  255.1 0.2 fusion.62
  255.3 0.0 copy-start.10
  255.3 2.5 multiply_reduce_fusion.3
  257.8 1.4 convolution_bitcast_fusion
  259.2 0.0 all-reduce.8.cloned.1.call-update
  259.2 145.0 %all-reduce.8.cloned.1.call-done = f32[2048,128]{0,1:T(8,128)} async-done(((f32[2048,128]{0,1:T(8,128)}), f32[2048,128]{0,1:T(8,128)}) %all-reduce.8.cloned.1.call-update) | async-done | bytes 1048592 | tf_op jit(solution)/shard_map/psum | solution.py:185
  404.2 2.5 copy.27
  (24 shorter events, 0.1 us)
Async XLA Ops:
  7.2 189.0 %copy-start = (bf16[512,2048]{1,0:T(8,128)(2,1)S(1)}, bf16[512,2048]{1,0:T(8,128)(2,1)}, u32[]{:S(2)}) copy-start(bf16[512,2048]{1,0:T(8,128)(2,1)} %param.22) | copy-start | bytes 6291460
  7.2 6.7 %copy-start.13 = (s32[8]{0:T(128)S(1)}, s32[8]{0:T(128)}, u32[]{:S(2)}) copy-start(s32[8]{0:T(128)} %param.17) | copy-start | bytes 100
  19.6 9.8 %copy-start.14 = (s32[1,32]{1,0:T(1,128)S(1)}, s32[1,32]{1,0:T(1,128)}, u32[]{:S(2)}) copy-start(s32[1,32]{1,0:T(1,128)} %param.18) | copy-start | bytes 388
  19.6 61.9 %all-to-all-start = ((bf16[32,32,2048]{2,1,0:T(8,128)(2,1)}), bf16[32,32,2048]{2,1,0:T(8,128)(2,1)}, u32[]{:S(2)}, u32[]{:S(2)}) async-start(bf16[32,32,2048]{2,1,0:T(8,128)(2,1)} %bitcast.142), calls=%async_computation | async-start | bytes 8388608 | tf_op jit(solution)/shard_map/all_to_all | solution.py:170
  91.1 9.8 %copy-start.3 = (bf16[2048,128]{1,0:T(8,128)(2,1)S(1)}, bf16[2048,128]{1,0:T(8,128)(2,1)}, u32[]{:S(2)}) copy-start(bf16[2048,128]{1,0:T(8,128)(2,1)} %param.30) | copy-start | bytes 1572868
  91.1 9.8 %copy-start.5 = (bf16[8,2048]{1,0:T(8,128)(2,1)S(1)}, bf16[8,2048]{1,0:T(8,128)(2,1)}, u32[]{:S(2)}) copy-start(bf16[8,2048]{1,0:T(8,128)(2,1)} %param.19) | copy-start | bytes 98308
  91.1 59.3 %all-to-all-start.1 = ((bf16[32,32,2048]{2,1,0:T(8,128)(2,1)}), bf16[32,32,2048]{2,1,0:T(8,128)(2,1)}, u32[]{:S(2)}, u32[]{:S(2)}) async-start(bf16[32,32,2048]{2,1,0:T(8,128)(2,1)} %broadcast_select_fusion), calls=%async_computation.1 | async-start | bytes 8388608 | tf_op jit(solution)/shard_map/all_to_all | solution.py:172
  98.3 305.9 %all-reduce.8.cloned.1.call-start = ((), (), s32[]{:S(2)}) async-start(), calls=%async_computation.2 | async-start | bytes 2097152 | tf_op jit(solution)/shard_map/psum | solution.py:185
  100.9 4.6 %copy-start.1 = (bf16[16384,128]{1,0:T(8,128)(2,1)S(1)}, bf16[16384,128]{1,0:T(8,128)(2,1)}, u32[]{:S(2)}) copy-start(bf16[16384,128]{1,0:T(8,128)(2,1)} %param.31) | copy-start | bytes 12582916
  160.6 15.2 %copy-start.8 = (f32[512]{0:T(512)S(1)}, f32[512]{0:T(512)}, u32[]{:S(2)}) copy-start(f32[512]{0:T(512)} %param.23) | copy-start | bytes 6148
  160.6 15.2 %copy-start.11 = (f32[512]{0:T(512)S(1)}, f32[512]{0:T(512)}, u32[]{:S(2)}) copy-start(f32[512]{0:T(512)} %param.24) | copy-start | bytes 6148
  175.9 8.1 %slice-start = ((s8[4718592]{0:T(1024)(128)(4,1)}), s8[4194304]{0:T(1024)(128)(4,1)S(1)}, s32[]{:S(2)}) async-start(s8[4718592]{0:T(1024)(128)(4,1)} %bitcast.143), calls=%async_computation.3 | async-start | bytes 8388608
  178.6 5.3 %slice-start.1 = ((s8[4718592]{0:T(1024)(128)(4,1)}), s8[524288]{0:T(1024)(128)(4,1)S(1)}, s32[]{:S(2)}) async-start(s8[4718592]{0:T(1024)(128)(4,1)} %bitcast.143), calls=%async_computation.4 | async-start | bytes 1048576
  187.5 8.6 %copy-start.9 = (f32[512]{0:T(512)S(1)}, f32[512]{0:T(512)}, u32[]{:S(2)}) copy-start(f32[512]{0:T(512)} %param.25) | copy-start | bytes 6148
  187.5 8.7 %copy-start.12 = (f32[512]{0:T(512)S(1)}, f32[512]{0:T(512)}, u32[]{:S(2)}) copy-start(f32[512]{0:T(512)} %param.26) | copy-start | bytes 6148
  196.2 20.4 %copy-start.6 = (f32[2048]{0:T(1024)S(1)}, f32[2048]{0:T(1024)}, u32[]{:S(2)}) copy-start(f32[2048]{0:T(1024)} %param.27) | copy-start | bytes 24580
  196.2 20.4 %copy-start.7 = (f32[2048]{0:T(1024)S(1)}, f32[2048]{0:T(1024)}, u32[]{:S(2)}) copy-start(f32[2048]{0:T(1024)} %param.28) | copy-start | bytes 24580
  216.6 5.9 %copy-start.4 = (bf16[2048,128]{1,0:T(8,128)(2,1)S(1)}, bf16[2048,128]{1,0:T(8,128)(2,1)}, u32[]{:S(2)}) copy-start(bf16[2048,128]{1,0:T(8,128)(2,1)} %param.29) | copy-start | bytes 1572868
  216.6 38.7 %copy-start.2 = (bf16[16384,128]{1,0:T(8,128)(2,1)S(1)}, bf16[16384,128]{1,0:T(8,128)(2,1)}, u32[]{:S(2)}) copy-start(bf16[16384,128]{1,0:T(8,128)(2,1)} %param.31) | copy-start | bytes 12582916
  255.3 151.5 %copy-start.10 = (bf16[8,128]{1,0:T(8,128)(2,1)}, bf16[8,128]{1,0:T(8,128)(2,1)S(1)}, u32[]{:S(2)}) copy-start(bf16[8,128]{1,0:T(8,128)(2,1)S(1)} %get-tuple-element.19) | copy-start | bytes 6148
Sparse Core Ops, SparseCore 0:
  259.3 144.8 all-reduce.7
where the time goes:
time: 414 us
  waiting for transfers between devices  239 us (58%)
  blocking collectives  59.2 us (14%)
  matrix products  43.1 us (10%)
  local copies, waits for them, and re-layouts  20.6 us (5%)
  other arithmetic  17.8 us (4%)
  starting transfers between devices  17 us (4%)
  between operations  16.3 us (4%)
    psum x1, waiting for transfers between devices, local(): query_grad = lax.psum(grad_part, ('dp', 'bn'))  145 us
    all_to_all x1, waiting for transfers between devices, local(): lax.all_to_all(pieces, 'dp', split_axis=0, concat_axis=0, tiled=True)  52 us
    all_to_all x1, waiting for transfers between devices, local(): lax.all_to_all(resent, 'dp', split_axis=0, concat_axis=0, tiled=True)  42.5 us
    all_gather x1, blocking collectives, local(): key_table = lax.all_gather(encoded, 'dp', axis=0, tiled=True)  32.2 us
    psum x3, blocking collectives, group_moments(): lax.psum((jnp.sum(values, axis=(0, 1, 2)), jnp.sum(values * values, axis=...  27 us
    dot_general x3, matrix products, time_conv(): jnp.einsum('afsc,cd->afsd', padded[:, offset:offset + length], weights[of...  16.8 us
    dot_general x9, matrix products, space_conv(): jnp.einsum('afhwc,cd->afhwd', window, weights[3 * row_shift + col_shift],...  11.5 us
    all_to_all x1, starting transfers between devices, local(): lax.all_to_all(pieces, 'dp', split_axis=0, concat_axis=0, tiled=True)  9.78 us
  transfers between devices with their start and end apart: 3, of which 3 were waited for; matrix products, arithmetic and copies ran while one was open for 2% of the time, Pallas kernels for 0%

commit v1 on v0

--- a/solution.py
+++ b/solution.py
@@ -163,23 +163,15 @@
     groups = lax.axis_size("bn")
     target = shuffle[0, lax.axis_index("dp")]
     row_count = groups * chosen.shape[0] * chosen.shape[1] * chosen.shape[2]
-    positions = jnp.arange(peer_count, dtype=jnp.int32)
-    matches = (shuffle[0][:, None] == positions[None, :]).astype(jnp.int32)
-    inverse = jnp.sum(positions[:, None] * matches, axis=0)
-    pieces = chosen.reshape((peer_count, -1, chosen.shape[3]))
-    relayed = lax.all_to_all(pieces, "dp", split_axis=0, concat_axis=0, tiled=True)
-    resent = jnp.take(relayed, inverse, axis=0)
-    arrived = lax.all_to_all(resent, "dp", split_axis=0, concat_axis=0, tiled=True)
-    hosted = arrived.reshape(chosen.shape)
+    slot = (jnp.arange(peer_count, dtype=jnp.int32) == target).astype(jnp.float32)
 
     def group_moments(values):
-        return lax.psum(
-            (jnp.sum(values, axis=(0, 1, 2)), jnp.sum(values * values, axis=(0, 1, 2))), "bn"
-        )
-
-    encoded = encode(hosted, params, group_moments, row_count)
-    key_table = lax.all_gather(encoded, "dp", axis=0, tiled=True)
-    own_keys = lax.dynamic_slice_in_dim(key_table, target * encoded.shape[0], encoded.shape[0], 0)
+        sums = jnp.stack([jnp.sum(values, axis=(0, 1, 2)), jnp.sum(values * values, axis=(0, 1, 2))])
+        table = lax.psum(slot[:, None, None] * sums[None], ("dp", "bn"))
+        own = lax.dynamic_index_in_dim(table, target, 0, keepdims=False)
+        return own[0], own[1]
+
+    own_keys = encode(chosen, params, group_moments, row_count)
     grad_proj = query_terms(query_feats, own_keys, w_query, queue)
     grad_part = jnp.einsum("nc,ne->ce", query_feats, grad_proj, preferred_element_type=jnp.float32)
     query_grad = lax.psum(grad_part, ("dp", "bn"))

time: 414 us -> 666 us (1.61)
  waiting for transfers between devices: 239 us -> 569 us
  blocking collectives: 59.2 us -> 0 us
  starting transfers between devices: 17 us -> 0.34 us
    psum x0 -> x3, waiting for transfers between devices: none -> 422 us  [group_moments(): table = lax.psum(slot[:, None, None] * sums[None], ('dp', 'bn'))]
    all_to_all x2 -> x0, waiting for transfers between devices: 94.4 us -> none  [the longest x1 52 us: local(): lax.all_to_all(pieces, 'dp', split_axis=0, concat_axis=0, tiled=True)]
    all_gather x1 -> x0, blocking collectives: 32.2 us -> none  [local(): key_table = lax.all_gather(encoded, 'dp', axis=0, tiled=True)]
    psum x3 -> x0, blocking collectives: 27 us -> none  [group_moments(): lax.psum((jnp.sum(values, axis=(0, 1, 2)), jnp.sum(values * values, axis=...]
    all_to_all x2 -> x0, starting transfers between devices: 17 us -> none  [the longest x1 9.78 us: local(): lax.all_to_all(pieces, 'dp', split_axis=0, concat_axis=0, tiled=True)]
  transfers between devices with their start and end apart: 3 -> 4, of which waited for: 3 -> 4; matrix products, arithmetic and copies ran while one was open for 2% -> 1% of each run, Pallas kernels for 0% -> 0%
where the time goes in v1:
time: 666 us
  waiting for transfers between devices  569 us (85%)
  matrix products  46 us (7%)
  other arithmetic  17.6 us (3%)
  local copies, waits for them, and re-layouts  16.1 us (2%)
  between operations  16.1 us (2%)
    psum x3, waiting for transfers between devices, group_moments(): table = lax.psum(slot[:, None, None] * sums[None], ('dp', 'bn'))  422 us
    psum x1, waiting for transfers between devices, local(): query_grad = lax.psum(grad_part, ('dp', 'bn'))  147 us
    dot_general x3, matrix products, time_conv(): jnp.einsum('afsc,cd->afsd', padded[:, offset:offset + length], weights[of...  19.6 us
  transfers between devices with their start and end apart: 4, of which 4 were waited for; matrix products, arithmetic and copies ran while one was open for 1% of the time, Pallas kernels for 0%

profile of v1, /device:TPU:1, one launch (start us, length us, event | category | flops | bytes accessed | tf_op | source)
XLA Modules:
  0.0 665.6 jit_solution(5777000886677736291)
XLA Ops:
  7.2 0.0 copy-start
  7.2 0.0 all-reduce.8.cloned.1.call-start
  7.2 6.7 %copy.18 = bf16[8,12,16,2048]{3,2,0,1:T(8,128)(2,1)} copy(bf16[8,12,16,2048]{3,2,1,0:T(8,128)(2,1)} %param.16) | data formatting | bytes 12582912 | tf_op args[0]
  14.0 5.6 gather_fusion
  19.5 6.7 %fusion.6 = f32[8,8,16,512]{3,2,1,0:T(8,128)} fusion(bf16[8,8,16,2048]{3,2,1,0:T(8,128)(2,1)} %gather_fusion, bf16[3,2048,512]{2,1,0:T(8,128)(2,1)} %param.20), kind=kOutput, calls=%fused_computation.13 | convolution fusion | flops 2147483648 | bytes 8388608 | tf_op jit(solution)/shard_map/afsc,cd->afsd/dot_general | solution.py:27
  26.2 0.0 copy-done.2
  26.2 5.2 fusion.8
  31.4 0.0 copy-done.14
  31.4 0.6 constant_dynamic-slice_fusion
  32.0 0.6 compare_convert_fusion
  32.7 0.0 copy-start.8
  32.7 0.0 copy-start.11
  32.7 7.7 %fusion.75 = (f32[512]{0:T(512)S(1)}, f32[512]{0:T(512)S(1)}, f32[8,8,16,512]{3,2,1,0:T(8,128)}) fusion(bf16[8,8,16,2048]{3,2,1,0:T(8,128)(2,1)} %gather_fusion, bf16[3,2048,512]{2,1,0:T(8,128)(2,1)} %param.20, f32[8,8,16,512]{3,2,1,0:T(8,128)} %fusion.8, f32[8,8,16,512]{3,2,1,0:T(8,128)} %fusion.6), kind=kOutput, calls=%fused_computation.113 | convolution fusion | flops 1881668608 | bytes 12587008 | tf_op jit(solution)/shard_map/afsc,cd->afsd/dot_general | solution.py:27
  40.4 0.8 broadcast_multiply_fusion.2
  41.2 0.0 all-reduce.8.cloned.1.call-update
  41.2 0.0 all-reduce.10.cloned.1.call-start
  43.2 143.4 %all-reduce.8.cloned.1.call-done = f32[32,2,512]{2,1,0:T(2,128)} async-done(((f32[32,2,512]{2,1,0:T(2,128)}), f32[32,2,512]{2,1,0:T(2,128)}) %all-reduce.8.cloned.1.call-update) | async-done | bytes 131088 | tf_op jit(solution)/shard_map/psum | solution.py:170
  186.6 0.8 dynamic-slice_multiply_fusion.5
  187.3 0.0 slice-start
  187.4 2.1 maximum_convert_fusion
  189.5 0.6 copy.37
  190.1 0.0 slice-start.1
  190.1 1.8 fusion.34
  191.9 1.7 fusion.36
  193.7 1.7 fusion.38
  195.4 0.7 fusion.40
  196.2 0.7 fusion.42
  196.9 0.7 fusion.44
  197.6 0.7 fusion.46
  198.3 0.7 fusion.48
  199.0 2.6 fusion.74
  201.7 0.8 broadcast_multiply_fusion.1
  202.4 0.0 all-reduce.10.cloned.1.call-update
  202.4 0.0 copy-start.9
  202.4 0.0 copy-start.12
  202.5 0.2 all-reduce.12.cloned.1.call-start
  202.7 3.9 fusion
  206.6 135.4 %all-reduce.10.cloned.1.call-done = f32[32,2,512]{2,1,0:T(2,128)} async-done(((f32[32,2,512]{2,1,0:T(2,128)}), f32[32,2,512]{2,1,0:T(2,128)}) %all-reduce.10.cloned.1.call-update) | async-done | bytes 131088 | tf_op jit(solution)/shard_map/psum | solution.py:170
  342.0 0.8 dynamic-slice_multiply_fusion.3
  342.8 0.0 copy-start.3
  342.8 0.0 copy-start.5
  342.8 0.0 copy-start.6
  342.8 0.0 copy-start.7
  342.9 8.0 %fusion.73 = (f32[2048]{0:T(1024)S(1)}, f32[2048]{0:T(1024)S(1)}, f32[8,8,16,2048]{3,2,1,0:T(8,128)}) fusion(bf16[512,2048]{1,0:T(8,128)(2,1)S(1)} %copy-done, f32[8,8,16,512]{3,1,2,0:T(8,128)} %bitcast.149, f32[512]{0:T(512)S(1)} %copy-done.12, f32[512]{0:T(512)S(1)} %rsqrt_multiply_fusion.1, f32[512]{0:T(512)S(1)} %bitcast.160), kind=kOutput, calls=%fused_computation.111 | convolution fusion | flops 2156392448 | bytes 12605440 | tf_op jit(solution)/shard_map/afsc,cd->afsd/dot_general | solution.py:83
  350.9 1.0 broadcast_multiply_fusion
  351.9 0.0 all-reduce.12.cloned.1.call-update
  351.9 0.0 all-reduce.14.cloned.1.call-start
  352.0 0.0 copy-done.3
  352.0 0.0 copy-done.5
  352.0 0.3 multiply_reduce_fusion.4
  352.3 143.6 %all-reduce.12.cloned.1.call-done = f32[32,2,2048]{2,1,0:T(2,128)} async-done(((f32[32,2,2048]{2,1,0:T(2,128)}), f32[32,2,2048]{2,1,0:T(2,128)}) %all-reduce.12.cloned.1.call-update) | async-done | bytes 524304 | tf_op jit(solution)/shard_map/psum | solution.py:170
  495.9 0.8 dynamic-slice_multiply_fusion.1
  496.8 0.0 copy-start.4
  496.8 0.0 copy-start.1
  496.8 5.8 maximum_reduce_fusion
  502.6 0.3 multiply_reduce_fusion.5
  503.0 2.5 exponential_reduce_fusion
  505.4 0.2 fusion.62
  505.6 0.0 copy-start.10
  505.6 2.5 multiply_reduce_fusion.3
  508.1 1.4 convolution_bitcast_fusion
  509.5 0.0 all-reduce.14.cloned.1.call-update
  509.6 147.0 %all-reduce.14.cloned.1.call-done = f32[2048,128]{0,1:T(8,128)} async-done(((f32[2048,128]{0,1:T(8,128)}), f32[2048,128]{0,1:T(8,128)}) %all-reduce.14.cloned.1.call-update) | async-done | bytes 1048592 | tf_op jit(solution)/shard_map/psum | solution.py:177
  656.5 2.5 copy.22
  (27 shorter events, 0.1 us)
Async XLA Ops:
  7.2 335.6 %copy-start = (bf16[512,2048]{1,0:T(8,128)(2,1)S(1)}, bf16[512,2048]{1,0:T(8,128)(2,1)}, u32[]{:S(2)}) copy-start(bf16[512,2048]{1,0:T(8,128)(2,1)} %param.22) | copy-start | bytes 6291460
  7.2 6.8 %copy-start.13 = (s32[8]{0:T(128)S(1)}, s32[8]{0:T(128)}, u32[]{:S(2)}) copy-start(s32[8]{0:T(128)} %param.17) | copy-start | bytes 100
  7.2 179.4 %all-reduce.8.cloned.1.call-start = ((), (), s32[]{:S(2)}) async-start(), calls=%async_computation | async-start | bytes 262144 | tf_op jit(solution)/shard_map/psum | solution.py:170
  19.5 6.7 %copy-start.2 = (bf16[8,8,16,2048]{3,2,1,0:T(8,128)(2,1)S(1)}, bf16[8,8,16,2048]{3,2,1,0:T(8,128)(2,1)}, u32[]{:S(2)}) copy-start(bf16[8,8,16,2048]{3,2,1,0:T(8,128)(2,1)} %gather_fusion) | copy-start | bytes 12582916
  26.2 5.2 copy-start.14
  32.7 154.6 %copy-start.8 = (f32[512]{0:T(512)S(1)}, f32[512]{0:T(512)}, u32[]{:S(2)}) copy-start(f32[512]{0:T(512)} %param.23) | copy-start | bytes 6148
  32.7 154.6 %copy-start.11 = (f32[512]{0:T(512)S(1)}, f32[512]{0:T(512)}, u32[]{:S(2)}) copy-start(f32[512]{0:T(512)} %param.24) | copy-start | bytes 6148
  41.2 300.8 %all-reduce.10.cloned.1.call-start = ((), (), s32[]{:S(2)}) async-start(), calls=%async_computation.1 | async-start | bytes 262144 | tf_op jit(solution)/shard_map/psum | solution.py:170
  187.3 8.1 %slice-start = ((s8[4718592]{0:T(1024)(128)(4,1)}), s8[4194304]{0:T(1024)(128)(4,1)S(1)}, s32[]{:S(2)}) async-start(s8[4718592]{0:T(1024)(128)(4,1)} %bitcast.147), calls=%async_computation.4 | async-start | bytes 8388608
  190.1 5.3 slice-start.1
  202.4 140.3 %copy-start.9 = (f32[512]{0:T(512)S(1)}, f32[512]{0:T(512)}, u32[]{:S(2)}) copy-start(f32[512]{0:T(512)} %param.25) | copy-start | bytes 6148
  202.4 140.3 %copy-start.12 = (f32[512]{0:T(512)S(1)}, f32[512]{0:T(512)}, u32[]{:S(2)}) copy-start(f32[512]{0:T(512)} %param.26) | copy-start | bytes 6148
  202.5 293.5 %all-reduce.12.cloned.1.call-start = ((), (), s32[]{:S(2)}) async-start(), calls=%async_computation.2 | async-start | bytes 1048576 | tf_op jit(solution)/shard_map/psum | solution.py:170
  342.8 9.2 %copy-start.3 = (bf16[2048,128]{1,0:T(8,128)(2,1)S(1)}, bf16[2048,128]{1,0:T(8,128)(2,1)}, u32[]{:S(2)}) copy-start(bf16[2048,128]{1,0:T(8,128)(2,1)} %param.30) | copy-start | bytes 1572868
  342.8 9.2 %copy-start.5 = (bf16[8,2048]{1,0:T(8,128)(2,1)S(1)}, bf16[8,2048]{1,0:T(8,128)(2,1)}, u32[]{:S(2)}) copy-start(bf16[8,2048]{1,0:T(8,128)(2,1)} %param.19) | copy-start | bytes 98308
  342.8 153.9 %copy-start.6 = (f32[2048]{0:T(1024)S(1)}, f32[2048]{0:T(1024)}, u32[]{:S(2)}) copy-start(f32[2048]{0:T(1024)} %param.27) | copy-start | bytes 24580
  342.8 153.9 %copy-start.7 = (f32[2048]{0:T(1024)S(1)}, f32[2048]{0:T(1024)}, u32[]{:S(2)}) copy-start(f32[2048]{0:T(1024)} %param.28) | copy-start | bytes 24580
  351.9 304.6 %all-reduce.14.cloned.1.call-start = ((), (), s32[]{:S(2)}) async-start(), calls=%async_computation.3 | async-start | bytes 2097152 | tf_op jit(solution)/shard_map/psum | solution.py:177
  496.8 5.9 copy-start.4
  496.8 6.2 copy-start.1
  505.6 2.5 copy-start.10
Sparse Core Ops, SparseCore 0:
  41.3 145.2 all-reduce.7
  202.6 139.4 all-reduce.9
  352.0 143.8 all-reduce.11
  509.7 146.7 all-reduce.13

commit v2 on v1

v2 whole, which is shorter than its diff:
```python
import jax
import jax.numpy as jnp
from jax import lax
from jax.experimental import pallas as pl
from jax.experimental.pallas import tpu as pltpu
from jax.sharding import PartitionSpec as P

MESH = pl.DeviceIdType.MESH
F32, BF16, I32 = jnp.float32, jnp.bfloat16, jnp.int32
CLIPS, FRAMES, TF, SPOTS, SIDE = 8, 8, 12, 16, 4
C, INNER, EMB, QUEUE = 2048, 512, 128, 16384
PLANE, LINE, PEERS = 16, 8, 32
KC = 512
NK = C // KC
ROWS = CLIPS * FRAMES * SPOTS
COUNT = float(4 * ROWS)
EPS, TINY = 1e-05, 1e-06
PARTS = ((0, 640), (640, 640), (1280, 768))
ORDER = ((2, 1, 0), (1, 0, 2), (0, 2, 1))


def await_bytes(ref, sem):
    pltpu.make_async_copy(ref, ref, sem).wait()


def kernel(
    starts, feats, shuf, qf_h, wt_h, ws_h, we_h, g1, s1, g2, s2, g3, s3, wk_h, wq_h, queue_h,
    keys_out, grad_out,
    xall, xc, wt, acc, act, ws, act2, we, third, queue_v, qall, qt, wk, wq,
    tabv, tabs, picks, sb1, sb3, ra1, ra3, tb1, tb3, rb1, rb3, qmine, gall, pooled, gvec,
    hsem, asem, bsem, gsem, tsem, qsem, csem,
):
    i, x = lax.axis_index("dp"), lax.axis_index("bn")
    yz, core = i // 2, i % 2
    y, z = yz // 4, yz % 4
    xyz = (x, y, z)
    member = x * 2 + core
    half = core * 4 + x
    gall_plane = gall.at[0, pl.ds(0, PLANE - 1)]
    gall_line = gall.at[pl.ds(0, LINE - 1)]

    def plane_peer(k):
        return ((yz + k) % PLANE * 2 + core, x)

    def line_peer(k):
        m = (member + k) % LINE
        return (yz * 2 + m % 2, m // 2)

    def axis_peer(axis, k):
        c = list(xyz)
        c[axis] = (c[axis] + k) % 4
        return ((c[1] * 4 + c[2]) * 2 + core, c[0])

    barrier = pltpu.get_barrier_semaphore()
    for k in range(1, PLANE):
        pl.semaphore_signal(barrier, inc=1, device_id=plane_peer(k), device_id_type=MESH)
    for k in range(1, LINE):
        pl.semaphore_signal(barrier, inc=1, device_id=line_peer(k), device_id_type=MESH)

    def load(src, dst, n):
        return pltpu.make_async_copy(src, dst, hsem.at[n])

    own_q = qall.at[core, x, y, z]
    feat_loads = [load(feats.at[:, :, :, pl.ds(KC * k, KC)], xall[k], k) for k in range(NK)]
    wt_loads = [load(wt_h.at[:, pl.ds(KC * k, KC), :], wt.at[k], NK + k) for k in range(NK)]
    small = [load(qf_h, own_q, 8), load(qf_h, qmine, 9), load(wq_h, wq, 10)]
    queue_load = load(queue_h, queue_v, 11)
    ws_load = load(ws_h, ws, 12)
    we_load = load(we_h, we, 13)
    wk_load = load(wk_h, wk, 14)
    for k in range(2):
        feat_loads[k].start()
        wt_loads[k].start()
    for d in small:
        d.start()

    row = shuf[...].astype(F32)
    sq = (PEERS, PEERS)
    r_i = lax.broadcasted_iota(I32, sq, 0)
    c_i = lax.broadcasted_iota(I32, sq, 1)
    wide = jnp.broadcast_to(row, sq)
    column = jnp.sum(jnp.where(r_i == c_i, wide, 0.0), axis=1, keepdims=True)
    hit = column == c_i.astype(F32)
    inverse = jnp.sum(jnp.where(hit, r_i.astype(F32), 0.0), axis=0, keepdims=True)
    tabv[x] = jnp.zeros((8, 128), I32)
    tabv[4] = jnp.zeros((8, 128), I32)
    tabv[x, 0:1, 0:PEERS] = shuf[...]
    tabv[4, 0:1, 0:PEERS] = inverse.astype(I32)

    for k in range(NK):
        for e in (0, FRAMES + 1):
            xc[k, :, e] = jnp.zeros((CLIPS, SPOTS, KC), BF16)

    def conv_one(k):
        def pick(n, _):
            first = starts[n]
            for t in range(FRAMES):
                xc[k, n, 1 + t] = xall[k][n, first + t]
            return 0

        lax.fori_loop(0, CLIPS, pick, 0)

        def rows(p, _):
            lhs = jnp.concatenate(
                [xc[k, pl.ds(2 * p, 2), o : o + FRAMES].reshape(256, KC) for o in range(3)], axis=1
            )
            r = jnp.dot(lhs, wt[k].reshape(3 * KC, INNER), preferred_element_type=F32)
            at = pl.ds(pl.multiple_of(p * 256, 256), 256)
            for q in range(4):
                v = r[:, 128 * q : 128 * (q + 1)]
                acc[q, at, :] = v if k == 0 else acc[q, at, :] + v
            return 0

        lax.fori_loop(0, CLIPS // 2, rows, 0)

    def q_region(p, done):
        at = [pl.ds(xyz[a], 1) for a in range(3)]
        for a in done:
            at[a] = pl.ds(0, 4)
        return qall.at[(core, *at, slice(None), pl.ds(*PARTS[p]))]

    def q_send(phase):
        for p in range(3):
            part = q_region(p, ORDER[p][:phase])
            for k in range(1, 4):
                pltpu.make_async_remote_copy(
                    src_ref=part, dst_ref=part, send_sem=qsem.at[0, p, phase], recv_sem=qsem.at[1, p, phase],
                    device_id=axis_peer(ORDER[p][phase], k), device_id_type=MESH,
                ).start()

    def q_wait(phase, side):
        for p in range(3):
            cols = pl.ds(*PARTS[p])
            ref = (
                qall.at[0, 0, 0, pl.ds(0, 3), :, cols],
                qall.at[0, 0, pl.ds(0, 3), :, :, cols],
                qall.at[0, pl.ds(0, 3), :, :, :, cols],
            )[phase]
            await_bytes(ref, qsem.at[side, p, phase])

    core_copy = pltpu.make_async_remote_copy(
        src_ref=qall.at[core], dst_ref=qall.at[core], send_sem=csem.at[0], recv_sem=csem.at[1],
        device_id=(yz * 2 + 1 - core, x), device_id_type=MESH,
    )

    def plane_send(r, sb, ra):
        for k in range(1, PLANE):
            pltpu.make_async_remote_copy(
                src_ref=sb.at[...], dst_ref=ra.at[k - 1], send_sem=asem.at[0, r], recv_sem=asem.at[1, r],
                device_id=plane_peer(k), device_id_type=MESH,
            ).start()

    def plane_finish(r, sb, ra, tb, rb):
        ra[PLANE - 1] = sb[...]
        await_bytes(ra.at[pl.ds(0, PLANE - 1)], asem.at[1, r])
        mine = None
        for k in range(LINE):
            v = ra[picks[0, k]] * jnp.where(picks[1, k] == 1, 1.0, 0.0).astype(F32)
            if k == 0:
                mine = v
                continue
            tb[k - 1] = v
            pltpu.make_async_remote_copy(
                src_ref=tb.at[k - 1], dst_ref=rb.at[k - 1], send_sem=bsem.at[0, r], recv_sem=bsem.at[1, r],
                device_id=line_peer(k), device_id_type=MESH,
            ).start()
        await_bytes(rb.at[pl.ds(0, LINE - 1)], bsem.at[1, r])
        for k in range(LINE - 1):
            mine = mine + rb[k]
        return mine

    def put_stats(dst, total, squares):
        for q in range(4):
            dst[q : q + 1, :] = total[:, 128 * q : 128 * (q + 1)]
            dst[4 + q : 5 + q, :] = squares[:, 128 * q : 128 * (q + 1)]

    def affine(tile, gain, shift):
        scales, shifts = [], []
        for q in range(4):
            m = tile[q : q + 1, :] * (1.0 / COUNT)
            w = tile[4 + q : 5 + q, :] * (1.0 / COUNT) - m * m
            scale = gain[:, 128 * q : 128 * (q + 1)] * lax.rsqrt(w + EPS)
            scales.append(scale)
            shifts.append(shift[:, 128 * q : 128 * (q + 1)] - m * scale)
        return jnp.concatenate(scales, axis=1), jnp.concatenate(shifts, axis=1)

    def sums_of(block):
        v = block.reshape(-1, 8, INNER)
        return jnp.sum(v, axis=0), jnp.sum(v * v, axis=0)

    def rows_of(ref, at):
        return jnp.concatenate([ref[q, at, :] for q in range(4)], axis=1)

    def total_of(ref):
        def body(p, carry):
            a, b = sums_of(rows_of(ref, pl.ds(pl.multiple_of(p * 128, 128), 128)))
            return carry[0] + a, carry[1] + b

        zero = jnp.zeros((8, INNER), F32)
        a, b = lax.fori_loop(0, ROWS // 128, body, (zero, zero))
        return jnp.sum(a, axis=0, keepdims=True), jnp.sum(b, axis=0, keepdims=True)

    for k in range(NK):
        feat_loads[k].wait()
        wt_loads[k].wait()
        if k + 2 < NK:
            feat_loads[k + 2].start()
            wt_loads[k + 2].start()
        if k == 1:
            queue_load.start()
            ws_load.start()
        if k == 2:
            we_load.start()
            wk_load.start()
        conv_one(k)
        if k == 0:
            pl.semaphore_wait(barrier, PLANE - 1 + LINE - 1)
            for d in small:
                d.wait()
            for n in range(1, 4):
                pltpu.make_async_remote_copy(
                    src_ref=tabv.at[x], dst_ref=tabv.at[x], send_sem=tsem.at[0], recv_sem=tsem.at[1],
                    device_id=axis_peer(0, n), device_id_type=MESH,
                ).start()
            q_send(0)
        if k == 2:
            q_wait(0, 1)
            q_send(1)
    put_stats(sb1.at[0, 0], *total_of(acc))
    plane_send(0, sb1.at[0], ra1[0])

    await_bytes(tabv.at[pl.ds(0, 3)], tsem.at[1])
    to_scalar = pltpu.make_async_copy(tabv, tabs, hsem.at[15])
    to_scalar.start()
    to_scalar.wait()
    for k in range(LINE):
        m = (member + k) % LINE
        group = tabs[m // 2, 0, yz * 2 + m % 2]
        j = tabs[4, 0, group]
        picks[0, k] = (yz - j // 2 + PLANE - 1) % PLANE
        picks[1, k] = jnp.where(j % 2 == core, 1, 0).astype(I32)

    zq = jnp.dot(qmine[...], wq[...], preferred_element_type=F32)
    length = jnp.sqrt(jnp.sum(zq * zq, axis=-1, keepdims=True) + TINY)
    unit = zq / length
    unit_b = unit.astype(BF16)
    queue_load.wait()

    def queue_part(lo, hi, carry):
        def body(n, carry):
            total, mix = carry
            qb = queue_v[pl.ds(pl.multiple_of(n * 1024, 1024), 1024), :].astype(F32)
            inv = lax.rsqrt(jnp.sum(qb * qb, axis=-1, keepdims=True) + TINY)
            qu = (qb * inv).astype(BF16)
            neg = lax.dot_general(unit_b, qu, (((1,), (1,)), ((), ())), preferred_element_type=F32) * 5.0
            e = jnp.exp(neg)
            total = total + jnp.sum(e, axis=-1, keepdims=True)
            mix = mix + jnp.dot(e.astype(BF16), qu, preferred_element_type=F32)
            return total, mix

        return lax.fori_loop(lo, hi, body, carry)

    carry = (jnp.zeros((CLIPS, 1), F32), jnp.zeros((CLIPS, EMB), F32))
    carry = queue_part(0, 8, carry)

    tile = plane_finish(0, sb1.at[0], ra1[0], tb1.at[0], rb1.at[0])
    q_wait(1, 1)
    q_send(2)

    scale, shift = affine(tile[0], g1[...], s1[...])
    for r in range(4):
        for e in (0, SIDE + 1):
            act[r, e] = jnp.zeros((64, INNER), BF16)

    def norm_one(p, _):
        for r in range(SIDE):
            for c in range(SIDE):
                both = [
                    rows_of(acc, pl.ds((2 * p + h) * 128 + SIDE * r + c, FRAMES, stride=SPOTS)) for h in range(2)
                ]
                v = jnp.concatenate(both, axis=0)
                v = jnp.maximum(v * scale + shift, 0.0).astype(BF16)
                act[r, c + 1, pl.ds(pl.multiple_of(p * 16, 16), 16), :] = v
        return 0

    lax.fori_loop(0, CLIPS // 2, norm_one, 0)

    ws_load.wait()

    def row_conv(r, base, tap, taps):
        lhs = jnp.concatenate(
            [act[base + d, c : c + SIDE].reshape(256, INNER) for d in range(taps) for c in range(3)], axis=1
        )
        w = ws[pl.ds(tap, 3 * taps)].reshape(3 * taps * INNER, INNER)
        v = jnp.dot(lhs, w, preferred_element_type=F32)
        for q in range(4):
            acc[q, pl.ds(pl.multiple_of(r * 256, 256), 256), :] = v[:, 128 * q : 128 * (q + 1)]

    def edge(n, _):
        row_conv(3 * n, 2 * n, 3 - 3 * n, 2)
        return 0

    def middle(n, _):
        row_conv(1 + n, n, 0, 3)
        return 0

    lax.fori_loop(0, 2, edge, 0)
    lax.fori_loop(0, 2, middle, 0)
    put_stats(sb1.at[1, 0], *total_of(acc))
    plane_send(1, sb1.at[1], ra1[1])
    carry = queue_part(8, 16, carry)
    tile = plane_finish(1, sb1.at[1], ra1[1], tb1.at[1], rb1.at[1])

    scale, shift = affine(tile[0], g2[...], s2[...])

    def norm_two(p, _):
        for h in range(8):
            v = rows_of(acc, pl.ds(p * 8 + h, SPOTS, stride=64))
            act2[pl.ds(pl.multiple_of(p * 128, 128) + h * 16, 16), :] = jnp.maximum(
                v * scale + shift, 0.0
            ).astype(BF16)
        return 0

    lax.fori_loop(0, CLIPS, norm_two, 0)
    we_load.wait()

    def expand(q, _):
        def body(p, carry):
            at = pl.ds(pl.multiple_of(p * 256, 256), 256)
            cols = pl.ds(pl.multiple_of(q * INNER, INNER), INNER)
            r = jnp.dot(act2[at, :], we[:, cols], preferred_element_type=F32)
            third[q, at, :] = r
            a, b = sums_of(r)
            return carry[0] + a, carry[1] + b

        zero = jnp.zeros((8, INNER), F32)
        a, b = lax.fori_loop(0, 4, body, (zero, zero))
        put_stats(sb3.at[q], jnp.sum(a, axis=0, keepdims=True), jnp.sum(b, axis=0, keepdims=True))
        return 0

    lax.fori_loop(0, 4, expand, 0)
    plane_send(2, sb3, ra3)
    q_wait(2, 1)
    core_copy.start()
    tile = plane_finish(2, sb3, ra3, tb3, rb3)

    for q in range(4):
        cols = slice(INNER * q, INNER * (q + 1))
        scale, shift = affine(tile[q], g3[:, cols], s3[:, cols])

        def pool(n, _):
            v = third[q, pl.ds(pl.multiple_of(n * 128, 128), 128), :]
            kept = xc[q, n, 1 : 1 + FRAMES].reshape(128, KC).astype(F32)
            v = jnp.maximum(v * scale + shift + kept, 0.0)
            part = jnp.sum(v.reshape(16, 8, INNER), axis=0)
            pooled[pl.ds(n, 1), cols] = jnp.sum(part, axis=0, keepdims=True) * (1.0 / 128.0)
            return 0

        lax.fori_loop(0, CLIPS, pool, 0)
    wk_load.wait()
    projected = jnp.dot(pooled[...].astype(BF16), wk[...], preferred_element_type=F32)
    norm = jnp.sum(projected * projected, axis=-1, keepdims=True) + TINY
    keys = (projected * lax.rsqrt(norm)).astype(BF16)
    keys_out[...] = keys

    held = keys.astype(F32)
    total, mix = carry
    e_pos = jnp.exp(jnp.sum(unit * held, axis=-1, keepdims=True) * 5.0)
    whole = e_pos + total
    grad = (mix / whole + (e_pos / whole - 1.0) * held) * 5.0
    radial = jnp.sum(unit * grad, axis=-1, keepdims=True)
    gvec[...] = ((grad - radial * unit) / length).astype(BF16)
    for k in range(1, PLANE):
        pltpu.make_async_remote_copy(
            src_ref=gvec, dst_ref=gall.at[half, yz], send_sem=gsem.at[0], recv_sem=gsem.at[1],
            device_id=plane_peer(k), device_id_type=MESH,
        ).start()
    gall[half, yz] = gvec[...]
    core_copy.wait_recv()

    def turn(n, _):
        cols = pl.ds(pl.multiple_of(n * 128, 128), 128)
        v = qall[:, :, :, :, :, cols].astype(F32).reshape(1024, 128)
        qt[cols, :] = v.T.astype(BF16)
        return 0

    lax.fori_loop(0, C // 128, turn, 0)
    await_bytes(gall_plane, gsem.at[1])
    for k in range(1, LINE):
        pltpu.make_async_remote_copy(
            src_ref=gall.at[half], dst_ref=gall.at[half], send_sem=gsem.at[2], recv_sem=gsem.at[3],
            device_id=line_peer(k), device_id_type=MESH,
        ).start()
    await_bytes(gall_line, gsem.at[3])
    g_all = gall[...].astype(F32).reshape(1024, EMB).astype(BF16)

    def last(n, _):
        at = pl.ds(pl.multiple_of(n * 256, 256), 256)
        grad_out[at, :] = jnp.dot(qt[at, :], g_all, preferred_element_type=F32)
        return 0

    lax.fori_loop(0, C // 256, last, 0)

    await_bytes(tabv.at[pl.ds(0, 3)], tsem.at[0])
    for phase in range(3):
        q_wait(phase, 0)
    core_copy.wait_send()
    for r, ra, rb in ((0, ra1[0], rb1.at[0]), (1, ra1[1], rb1.at[1]), (2, ra3, rb3)):
        await_bytes(ra.at[pl.ds(0, PLANE - 1)], asem.at[0, r])
        await_bytes(rb.at[pl.ds(0, LINE - 1)], bsem.at[0, r])
    await_bytes(gall_plane, gsem.at[0])
    await_bytes(gall_line, gsem.at[2])


def local(
    key_feats, clip_starts, shuffle, query_feats, conv_time, conv_space, conv_expand,
    gain_one, shift_one, gain_two, shift_two, gain_three, shift_three, w_key, w_query, queue,
):
    vmem = pl.BlockSpec(memory_space=pltpu.VMEM)
    smem = pl.BlockSpec(memory_space=pltpu.SMEM)
    hbm = pl.BlockSpec(memory_space=pltpu.HBM)
    V = pltpu.VMEM
    DMA = pltpu.SemaphoreType.DMA
    rows = [v.reshape(1, -1) for v in (gain_one, shift_one, gain_two, shift_two, gain_three, shift_three)]
    return pl.pallas_call(
        kernel,
        name="moco",
        out_shape=(
            jax.ShapeDtypeStruct((CLIPS, EMB), BF16),
            jax.ShapeDtypeStruct((C, EMB), F32),
        ),
        in_specs=[smem, hbm, vmem, hbm, hbm, hbm, hbm] + [vmem] * 6 + [hbm] * 3,
        out_specs=(vmem, vmem),
        scratch_shapes=[
            [V((CLIPS, TF, SPOTS, KC), BF16) for _ in range(NK)],
            V((NK, CLIPS, FRAMES + 2, SPOTS, KC), BF16),
            V((NK, 3, KC, INNER), BF16),
            V((4, ROWS, 128), F32),
            V((SIDE, SIDE + 2, 64, INNER), BF16),
            V((9, INNER, INNER), BF16),
            V((ROWS, INNER), BF16),
            V((INNER, C), BF16),
            V((4, ROWS, INNER), F32),
            V((QUEUE, EMB), BF16),
            V((2, 4, 4, 4, CLIPS, C), BF16),
            V((C, 1024), BF16),
            V((C, EMB), BF16),
            V((C, EMB), BF16),
            V((5, 8, 128), I32),
            pltpu.SMEM((5, 8, 128), I32),
            pltpu.SMEM((2, LINE), I32),
            V((2, 1, 8, 128), F32),
            V((4, 8, 128), F32),
            [V((PLANE, 1, 8, 128), F32) for _ in range(2)],
            V((PLANE, 4, 8, 128), F32),
            V((2, LINE - 1, 1, 8, 128), F32),
            V((LINE - 1, 4, 8, 128), F32),
            V((2, LINE - 1, 1, 8, 128), F32),
            V((LINE - 1, 4, 8, 128), F32),
            V((CLIPS, C), BF16),
            V((LINE, PLANE, CLIPS, EMB), BF16),
            V((CLIPS, C), F32),
            V((CLIPS, EMB), BF16),
            DMA((16,)),
            DMA((2, 3)),
            DMA((2, 3)),
            DMA((4,)),
            DMA((2,)),
            DMA((2, 3, 3)),
            DMA((2,)),
        ],
        compiler_params=pltpu.CompilerParams(
            collective_id=0, has_side_effects=True, vmem_limit_bytes=67043328
        ),
    )(
        clip_starts, key_feats, shuffle, query_feats, conv_time, conv_space, conv_expand,
        *rows, w_key, w_query, queue,
    )


def solution(mesh):
    placed = (
        (P(("dp", "bn"), None, None, None), P(("dp", "bn")), P("bn", None), P(("dp", "bn"), None)) + (P(),) * 12
    )
    return jax.shard_map(
        local, mesh=mesh, in_specs=placed, out_specs=(P(("dp", "bn"), None), P()), check_vma=False
    )
```

time: 666 us -> 81.1 us (0.12)
  waiting for transfers between devices: 569 us -> 0 us
  Pallas kernels: 0 us -> 76.7 us
  matrix products: 46 us -> 0 us
  other arithmetic: 17.6 us -> 0 us
  between operations: 16.1 us -> 0.65 us
  local copies, waits for them, and re-layouts: 16.1 us -> 3.52 us
    psum x4 -> x0, waiting for transfers between devices: 569 us -> none  [the longest x3 422 us: group_moments(): table = lax.psum(slot[:, None, None] * sums[None], ('dp', 'bn'))]
    pallas_call x0 -> x1, Pallas kernels: none -> 76.7 us  [local(): pl.pallas_call(kernel, name='moco', out_shape=(jax.ShapeDtypeStruct((CLIP...]
    dot_general x18 -> x0, matrix products: 46 us -> none  [the longest x3 19.6 us: time_conv(): jnp.einsum('afsc,cd->afsd', padded[:, offset:offset + length], weights[of...]
    reduce_sum x3 -> x0, other arithmetic: 9.93 us -> none  [the longest x1 5.82 us: encode(): pooled = jnp.mean(merged, axis=(1, 2)).astype(jnp.bfloat16)]
  transfers between devices with their start and end apart: 4 -> 0, of which waited for: 4 -> 0; matrix products, arithmetic and copies ran while one was open for 1% -> 0% of each run, Pallas kernels for 0% -> 0%
where the time goes in v2:
time: 81.1 us; the launch traced here: 80.9 us
  Pallas kernels  76.7 us (95%)
  local copies, waits for them, and re-layouts  3.52 us (4%)
    pallas_call x1, Pallas kernels, local(): pl.pallas_call(kernel, name='moco', out_shape=(jax.ShapeDtypeStruct((CLIP...  76.7 us
    unnamed x2, local copies, waits for them, and re-layouts  3.52 us

profile of v2, /device:TPU:1, one launch (start us, length us, event | category | flops | bytes accessed | tf_op | source)
XLA Modules:
  0.0 80.9 jit_solution(3272681286561331890)
XLA Ops:
  0.6 76.7 %moco.1 = (bf16[8,128]{1,0:T(8,128)(2,1)}, f32[2048,128]{1,0:T(8,128)}) custom-call(s32[8]{0:T(128)} %starts.1, bf16[8,12,16,2048]{3,2,1,0:T(8,128)(2,1)} %feats.1, s32[1,32]{1,0:T(1,128)} %shuf.1, bf16[8,2048]{1,0:T(8,128)(2,1)} %qf_h.1, bf16[3,2048,512]{2,1,0:T(8,128)(2,1)} %wt_h.1, bf16[9,512,512]{2,1,0:T(8,128)(2,1)} %ws_h.1, bf16[512,2048]{1,0:T(8,128)(2,1)} %we_h.1, ...), custom_call_target="tpu_custom_call" | custom-call | tf_op jit(solution)/shard_map/moco/pallas_call | solution.py:425
  77.4 1.3 %copy.20 = bf16[8,128]{1,0:T(8,128)(2,1)} copy(bf16[8,128]{1,0:T(8,128)(2,1)} %get-tuple-element.4) | data formatting | bytes 4096
  78.6 2.3 %copy.21 = f32[2048,128]{1,0:T(8,128)} copy(f32[2048,128]{1,0:T(8,128)} %get-tuple-element.5) | data formatting | bytes 2097152

commit v3 on v2

--- a/solution.py
+++ b/solution.py
@@ -9,7 +9,7 @@
 F32, BF16, I32 = jnp.float32, jnp.bfloat16, jnp.int32
 CLIPS, FRAMES, TF, SPOTS, SIDE = 8, 8, 12, 16, 4
 C, INNER, EMB, QUEUE = 2048, 512, 128, 16384
-PLANE, LINE, PEERS = 16, 8, 32
+PLANE, LINE, PEERS, ROUNDS = 16, 8, 32, 6
 KC = 512
 NK = C // KC
 ROWS = CLIPS * FRAMES * SPOTS
@@ -25,9 +25,9 @@
 
 def kernel(
     starts, feats, shuf, qf_h, wt_h, ws_h, we_h, g1, s1, g2, s2, g3, s3, wk_h, wq_h, queue_h,
-    keys_out, grad_out,
+    keys_out, qt_out, g_out,
     xall, xc, wt, acc, act, ws, act2, we, third, queue_v, qall, qt, wk, wq,
-    tabv, tabs, picks, sb1, sb3, ra1, ra3, tb1, tb3, rb1, rb3, qmine, gall, pooled, gvec,
+    tabv, tabs, picks, sb, ra, tb, rb, qmine, gall, pooled, gvec,
     hsem, asem, bsem, gsem, tsem, qsem, csem,
 ):
     i, x = lax.axis_index("dp"), lax.axis_index("bn")
@@ -66,13 +66,10 @@
     small = [load(qf_h, own_q, 8), load(qf_h, qmine, 9), load(wq_h, wq, 10)]
     queue_load = load(queue_h, queue_v, 11)
     ws_load = load(ws_h, ws, 12)
-    we_load = load(we_h, we, 13)
+    we_loads = [load(we_h.at[:, pl.ds(INNER * q, INNER)], we.at[q], 16 + q) for q in range(4)]
     wk_load = load(wk_h, wk, 14)
-    for k in range(2):
-        feat_loads[k].start()
-        wt_loads[k].start()
-    for d in small:
-        d.start()
+    feat_loads[0].start()
+    wt_loads[0].start()
 
     row = shuf[...].astype(F32)
     sq = (PEERS, PEERS)
@@ -102,16 +99,16 @@
 
         def rows(p, _):
             lhs = jnp.concatenate(
-                [xc[k, pl.ds(2 * p, 2), o : o + FRAMES].reshape(256, KC) for o in range(3)], axis=1
+                [xc[k, pl.ds(4 * p, 4), o : o + FRAMES].reshape(512, KC) for o in range(3)], axis=1
             )
             r = jnp.dot(lhs, wt[k].reshape(3 * KC, INNER), preferred_element_type=F32)
-            at = pl.ds(pl.multiple_of(p * 256, 256), 256)
+            at = pl.ds(pl.multiple_of(p * 512, 512), 512)
             for q in range(4):
                 v = r[:, 128 * q : 128 * (q + 1)]
                 acc[q, at, :] = v if k == 0 else acc[q, at, :] + v
             return 0
 
-        lax.fori_loop(0, CLIPS // 2, rows, 0)
+        lax.fori_loop(0, CLIPS // 4, rows, 0)
 
     def q_region(p, done):
         at = [pl.ds(xyz[a], 1) for a in range(3)]
@@ -143,36 +140,34 @@
         device_id=(yz * 2 + 1 - core, x), device_id_type=MESH,
     )
 
-    def plane_send(r, sb, ra):
+    def plane_send(r):
         for k in range(1, PLANE):
             pltpu.make_async_remote_copy(
-                src_ref=sb.at[...], dst_ref=ra.at[k - 1], send_sem=asem.at[0, r], recv_sem=asem.at[1, r],
+                src_ref=sb.at[r], dst_ref=ra[r].at[k - 1], send_sem=asem.at[0, r], recv_sem=asem.at[1, r],
                 device_id=plane_peer(k), device_id_type=MESH,
             ).start()
-
-    def plane_finish(r, sb, ra, tb, rb):
-        ra[PLANE - 1] = sb[...]
-        await_bytes(ra.at[pl.ds(0, PLANE - 1)], asem.at[1, r])
-        mine = None
-        for k in range(LINE):
-            v = ra[picks[0, k]] * jnp.where(picks[1, k] == 1, 1.0, 0.0).astype(F32)
-            if k == 0:
-                mine = v
-                continue
-            tb[k - 1] = v
+        ra[r][PLANE - 1] = sb[r]
+
+    def plane_forward(r):
+        await_bytes(ra[r].at[pl.ds(0, PLANE - 1)], asem.at[1, r])
+        for k in range(1, LINE):
+            tb[r, k - 1] = ra[r][picks[0, k]] * jnp.where(picks[1, k] == 1, 1.0, 0.0).astype(F32)
             pltpu.make_async_remote_copy(
-                src_ref=tb.at[k - 1], dst_ref=rb.at[k - 1], send_sem=bsem.at[0, r], recv_sem=bsem.at[1, r],
+                src_ref=tb.at[r, k - 1], dst_ref=rb.at[r, k - 1], send_sem=bsem.at[0, r], recv_sem=bsem.at[1, r],
                 device_id=line_peer(k), device_id_type=MESH,
             ).start()
-        await_bytes(rb.at[pl.ds(0, LINE - 1)], bsem.at[1, r])
+
+    def line_finish(r):
+        mine = ra[r][picks[0, 0]] * jnp.where(picks[1, 0] == 1, 1.0, 0.0).astype(F32)
+        await_bytes(rb.at[r, pl.ds(0, LINE - 1)], bsem.at[1, r])
         for k in range(LINE - 1):
-            mine = mine + rb[k]
+            mine = mine + rb[r, k]
         return mine
 
-    def put_stats(dst, total, squares):
+    def put_stats(r, parts):
         for q in range(4):
-            dst[q : q + 1, :] = total[:, 128 * q : 128 * (q + 1)]
-            dst[4 + q : 5 + q, :] = squares[:, 128 * q : 128 * (q + 1)]
+            sb[r, q : q + 1, :] = jnp.sum(parts[2 * q], axis=0, keepdims=True)
+            sb[r, 4 + q : 5 + q, :] = jnp.sum(parts[2 * q + 1], axis=0, keepdims=True)
 
     def affine(tile, gain, shift):
         scales, shifts = [], []
@@ -184,8 +179,10 @@
             shifts.append(shift[:, 128 * q : 128 * (q + 1)] - m * scale)
         return jnp.concatenate(scales, axis=1), jnp.concatenate(shifts, axis=1)
 
+    zeros = tuple(jnp.zeros((8, 128), F32) for _ in range(8))
+
     def sums_of(block):
-        v = block.reshape(-1, 8, INNER)
+        v = block.reshape(-1, 8, 128)
         return jnp.sum(v, axis=0), jnp.sum(v * v, axis=0)
 
     def rows_of(ref, at):
@@ -193,24 +190,30 @@
 
     def total_of(ref):
         def body(p, carry):
-            a, b = sums_of(rows_of(ref, pl.ds(pl.multiple_of(p * 128, 128), 128)))
-            return carry[0] + a, carry[1] + b
-
-        zero = jnp.zeros((8, INNER), F32)
-        a, b = lax.fori_loop(0, ROWS // 128, body, (zero, zero))
-        return jnp.sum(a, axis=0, keepdims=True), jnp.sum(b, axis=0, keepdims=True)
+            out = list(carry)
+            for q in range(4):
+                a, b = sums_of(ref[q, pl.ds(pl.multiple_of(p * 128, 128), 128), :])
+                out[2 * q] = out[2 * q] + a
+                out[2 * q + 1] = out[2 * q + 1] + b
+            return tuple(out)
+
+        return lax.fori_loop(0, ROWS // 128, body, zeros)
 
     for k in range(NK):
         feat_loads[k].wait()
         wt_loads[k].wait()
-        if k + 2 < NK:
-            feat_loads[k + 2].start()
-            wt_loads[k + 2].start()
-        if k == 1:
+        if k == 0:
+            for d in small:
+                d.start()
+        if k + 1 < NK:
+            feat_loads[k + 1].start()
+            wt_loads[k + 1].start()
+        if k == 2:
             queue_load.start()
             ws_load.start()
-        if k == 2:
-            we_load.start()
+        if k == 3:
+            for d in we_loads:
+                d.start()
             wk_load.start()
         conv_one(k)
         if k == 0:
@@ -226,8 +229,8 @@
         if k == 2:
             q_wait(0, 1)
             q_send(1)
-    put_stats(sb1.at[0, 0], *total_of(acc))
-    plane_send(0, sb1.at[0], ra1[0])
+    put_stats(0, total_of(acc))
+    plane_send(0)
 
     await_bytes(tabv.at[pl.ds(0, 3)], tsem.at[1])
     to_scalar = pltpu.make_async_copy(tabv, tabs, hsem.at[15])
@@ -263,11 +266,12 @@
     carry = (jnp.zeros((CLIPS, 1), F32), jnp.zeros((CLIPS, EMB), F32))
     carry = queue_part(0, 8, carry)
 
-    tile = plane_finish(0, sb1.at[0], ra1[0], tb1.at[0], rb1.at[0])
+    plane_forward(0)
+    tile = line_finish(0)
     q_wait(1, 1)
     q_send(2)
 
-    scale, shift = affine(tile[0], g1[...], s1[...])
+    scale, shift = affine(tile, g1[...], s1[...])
     for r in range(4):
         for e in (0, SIDE + 1):
             act[r, e] = jnp.zeros((64, INNER), BF16)
@@ -306,12 +310,13 @@
 
     lax.fori_loop(0, 2, edge, 0)
     lax.fori_loop(0, 2, middle, 0)
-    put_stats(sb1.at[1, 0], *total_of(acc))
-    plane_send(1, sb1.at[1], ra1[1])
+    put_stats(1, total_of(acc))
+    plane_send(1)
     carry = queue_part(8, 16, carry)
-    tile = plane_finish(1, sb1.at[1], ra1[1], tb1.at[1], rb1.at[1])
-
-    scale, shift = affine(tile[0], g2[...], s2[...])
+    plane_forward(1)
+    tile = line_finish(1)
+
+    scale, shift = affine(tile, g2[...], s2[...])
 
     def norm_two(p, _):
         for h in range(8):
@@ -322,43 +327,48 @@
         return 0
 
     lax.fori_loop(0, CLIPS, norm_two, 0)
-    we_load.wait()
-
-    def expand(q, _):
-        def body(p, carry):
-            at = pl.ds(pl.multiple_of(p * 256, 256), 256)
-            cols = pl.ds(pl.multiple_of(q * INNER, INNER), INNER)
-            r = jnp.dot(act2[at, :], we[:, cols], preferred_element_type=F32)
-            third[q, at, :] = r
-            a, b = sums_of(r)
-            return carry[0] + a, carry[1] + b
-
-        zero = jnp.zeros((8, INNER), F32)
-        a, b = lax.fori_loop(0, 4, body, (zero, zero))
-        put_stats(sb3.at[q], jnp.sum(a, axis=0, keepdims=True), jnp.sum(b, axis=0, keepdims=True))
-        return 0
-
-    lax.fori_loop(0, 4, expand, 0)
-    plane_send(2, sb3, ra3)
+    for d in we_loads:
+        d.wait()
+
+    for q in range(4):
+
+        def expand(p, carry):
+            at = pl.ds(pl.multiple_of(p * 512, 512), 512)
+            v = jnp.dot(act2[at, :], we[q], preferred_element_type=F32)
+            third[q, at, :] = v
+            out = list(carry)
+            for c in range(4):
+                a, b = sums_of(v[:, 128 * c : 128 * (c + 1)])
+                out[2 * c] = out[2 * c] + a
+                out[2 * c + 1] = out[2 * c + 1] + b
+            return tuple(out)
+
+        put_stats(2 + q, lax.fori_loop(0, 2, expand, zeros))
+        plane_send(2 + q)
     q_wait(2, 1)
     core_copy.start()
-    tile = plane_finish(2, sb3, ra3, tb3, rb3)
+    for q in range(4):
+        plane_forward(2 + q)
 
     for q in range(4):
         cols = slice(INNER * q, INNER * (q + 1))
-        scale, shift = affine(tile[q], g3[:, cols], s3[:, cols])
+        scale, shift = affine(line_finish(2 + q), g3[:, cols], s3[:, cols])
 
         def pool(n, _):
-            v = third[q, pl.ds(pl.multiple_of(n * 128, 128), 128), :]
-            kept = xc[q, n, 1 : 1 + FRAMES].reshape(128, KC).astype(F32)
-            v = jnp.maximum(v * scale + shift + kept, 0.0)
-            part = jnp.sum(v.reshape(16, 8, INNER), axis=0)
-            pooled[pl.ds(n, 1), cols] = jnp.sum(part, axis=0, keepdims=True) * (1.0 / 128.0)
+            at = pl.ds(pl.multiple_of(n * 128, 128), 128)
+            for c in range(4):
+                lanes = slice(128 * c, 128 * (c + 1))
+                kept = xc[q, n, 1 : 1 + FRAMES, :, lanes].reshape(128, 128).astype(F32)
+                v = jnp.maximum(third[q, at, lanes] * scale[:, lanes] + shift[:, lanes] + kept, 0.0)
+                pooled[n, :, INNER * q + 128 * c : INNER * q + 128 * (c + 1)] = jnp.sum(
+                    v.reshape(16, 8, 128), axis=0
+                )
             return 0
 
         lax.fori_loop(0, CLIPS, pool, 0)
     wk_load.wait()
-    projected = jnp.dot(pooled[...].astype(BF16), wk[...], preferred_element_type=F32)
+    mean = jnp.sum(pooled[...], axis=1) * (1.0 / 128.0)
+    projected = jnp.dot(mean.astype(BF16), wk[...], preferred_element_type=F32)
     norm = jnp.sum(projected * projected, axis=-1, keepdims=True) + TINY
     keys = (projected * lax.rsqrt(norm)).astype(BF16)
     keys_out[...] = keys
@@ -385,31 +395,34 @@
         return 0
 
     lax.fori_loop(0, C // 128, turn, 0)
+    qt_store = load(qt, qt_out, 15)
+    qt_store.start()
     await_bytes(gall_plane, gsem.at[1])
+    own_half = pltpu.make_async_copy(gall.at[half], g_out.at[half], hsem.at[13])
+    own_half.start()
     for k in range(1, LINE):
         pltpu.make_async_remote_copy(
-            src_ref=gall.at[half], dst_ref=gall.at[half], send_sem=gsem.at[2], recv_sem=gsem.at[3],
+            src_ref=gall.at[half], dst_ref=g_out.at[half], send_sem=gsem.at[2], recv_sem=gsem.at[3],
             device_id=line_peer(k), device_id_type=MESH,
         ).start()
     await_bytes(gall_line, gsem.at[3])
-    g_all = gall[...].astype(F32).reshape(1024, EMB).astype(BF16)
-
-    def last(n, _):
-        at = pl.ds(pl.multiple_of(n * 256, 256), 256)
-        grad_out[at, :] = jnp.dot(qt[at, :], g_all, preferred_element_type=F32)
-        return 0
-
-    lax.fori_loop(0, C // 256, last, 0)
+    own_half.wait()
+    qt_store.wait()
 
     await_bytes(tabv.at[pl.ds(0, 3)], tsem.at[0])
     for phase in range(3):
         q_wait(phase, 0)
     core_copy.wait_send()
-    for r, ra, rb in ((0, ra1[0], rb1.at[0]), (1, ra1[1], rb1.at[1]), (2, ra3, rb3)):
-        await_bytes(ra.at[pl.ds(0, PLANE - 1)], asem.at[0, r])
-        await_bytes(rb.at[pl.ds(0, LINE - 1)], bsem.at[0, r])
+    for r in range(ROUNDS):
+        await_bytes(ra[r].at[pl.ds(0, PLANE - 1)], asem.at[0, r])
+        await_bytes(rb.at[r, pl.ds(0, LINE - 1)], bsem.at[0, r])
     await_bytes(gall_plane, gsem.at[0])
     await_bytes(gall_line, gsem.at[2])
+
+
+def last(keys_ref, q_ref, g_ref, keys_out, grad_out):
+    keys_out[...] = keys_ref[...]
+    grad_out[...] = jnp.dot(q_ref[...], g_ref[...], preferred_element_type=F32)
 
 
 def local(
@@ -422,15 +435,16 @@
     V = pltpu.VMEM
     DMA = pltpu.SemaphoreType.DMA
     rows = [v.reshape(1, -1) for v in (gain_one, shift_one, gain_two, shift_two, gain_three, shift_three)]
-    return pl.pallas_call(
+    keys, q_t, grads = pl.pallas_call(
         kernel,
         name="moco",
         out_shape=(
             jax.ShapeDtypeStruct((CLIPS, EMB), BF16),
-            jax.ShapeDtypeStruct((C, EMB), F32),
+            jax.ShapeDtypeStruct((C, 1024), BF16),
+            jax.ShapeDtypeStruct((LINE, PLANE, CLIPS, EMB), BF16),
         ),
         in_specs=[smem, hbm, vmem, hbm, hbm, hbm, hbm] + [vmem] * 6 + [hbm] * 3,
-        out_specs=(vmem, vmem),
+        out_specs=(vmem, hbm, hbm),
         scratch_shapes=[
             [V((CLIPS, TF, SPOTS, KC), BF16) for _ in range(NK)],
             V((NK, CLIPS, FRAMES + 2, SPOTS, KC), BF16),
@@ -439,7 +453,7 @@
             V((SIDE, SIDE + 2, 64, INNER), BF16),
             V((9, INNER, INNER), BF16),
             V((ROWS, INNER), BF16),
-            V((INNER, C), BF16),
+            V((4, INNER, INNER), BF16),
             V((4, ROWS, INNER), F32),
             V((QUEUE, EMB), BF16),
             V((2, 4, 4, 4, CLIPS, C), BF16),
@@ -449,21 +463,17 @@
             V((5, 8, 128), I32),
             pltpu.SMEM((5, 8, 128), I32),
             pltpu.SMEM((2, LINE), I32),
-            V((2, 1, 8, 128), F32),
-            V((4, 8, 128), F32),
-            [V((PLANE, 1, 8, 128), F32) for _ in range(2)],
-            V((PLANE, 4, 8, 128), F32),
-            V((2, LINE - 1, 1, 8, 128), F32),
-            V((LINE - 1, 4, 8, 128), F32),
-            V((2, LINE - 1, 1, 8, 128), F32),
-            V((LINE - 1, 4, 8, 128), F32),
+            V((ROUNDS, 8, 128), F32),
+            [V((PLANE, 8, 128), F32) for _ in range(ROUNDS)],
+            V((ROUNDS, LINE - 1, 8, 128), F32),
+            V((ROUNDS, LINE - 1, 8, 128), F32),
             V((CLIPS, C), BF16),
             V((LINE, PLANE, CLIPS, EMB), BF16),
-            V((CLIPS, C), F32),
+            V((CLIPS, 8, C), F32),
             V((CLIPS, EMB), BF16),
-            DMA((16,)),
-            DMA((2, 3)),
-            DMA((2, 3)),
+            DMA((20,)),
+            DMA((2, ROUNDS)),
+            DMA((2, ROUNDS)),
             DMA((4,)),
             DMA((2,)),
             DMA((2, 3, 3)),
@@ -476,6 +486,19 @@
         clip_starts, key_feats, shuffle, query_feats, conv_time, conv_space, conv_expand,
         *rows, w_key, w_query, queue,
     )
+    tall = C // 4
+    return pl.pallas_call(
+        last,
+        name="last",
+        grid=(4,),
+        out_shape=(jax.ShapeDtypeStruct((CLIPS, EMB), BF16), jax.ShapeDtypeStruct((C, EMB), F32)),
+        in_specs=[
+            pl.BlockSpec((CLIPS, EMB), lambda n: (0, 0)),
+            pl.BlockSpec((tall, 1024), lambda n: (n, 0)),
+            pl.BlockSpec((1024, EMB), lambda n: (0, 0)),
+        ],
+        out_specs=(pl.BlockSpec((CLIPS, EMB), lambda n: (0, 0)), pl.BlockSpec((tall, EMB), lambda n: (n, 0))),
+    )(keys, q_t, grads.reshape(1024, EMB))
 
 
 def solution(mesh):

time: 81.1 us -> 73.3 us (0.904)
  Pallas kernels: 76.7 us -> 72.4 us
  local copies, waits for them, and re-layouts: 3.52 us -> 0 us
    pallas_call x1, Pallas kernels: 76.7 us -> 67.6 us  [local(): pl.pallas_call(kernel, name='moco', out_shape=(jax.ShapeDtypeStruct((CLIP...]
    pallas_call x0 -> x1, Pallas kernels: none -> 4.87 us  [local(): pl.pallas_call(last, name='last', grid=(4,), out_shape=(jax.ShapeDtypeStr...]
    unnamed x2 -> x0, local copies, waits for them, and re-layouts: 3.52 us -> none
where the time goes in v3:
time: 73.3 us; the launch traced here: 73.1 us
  Pallas kernels  72.4 us (99%)
    pallas_call x1, Pallas kernels, local(): pl.pallas_call(kernel, name='moco', out_shape=(jax.ShapeDtypeStruct((CLIP...  67.6 us
    pallas_call x1, Pallas kernels, local(): pl.pallas_call(last, name='last', grid=(4,), out_shape=(jax.ShapeDtypeStr...  4.87 us

profile of v3, /device:TPU:1, one launch (start us, length us, event | category | flops | bytes accessed | tf_op | source)
XLA Modules:
  0.0 73.1 jit_solution(18104052536738531961)
XLA Ops:
  0.6 67.6 %moco.1 = (bf16[8,128]{1,0:T(8,128)(2,1)}, bf16[2048,1024]{1,0:T(8,128)(2,1)}, bf16[8,16,8,128]{3,2,1,0:T(8,128)(2,1)}) custom-call(s32[8]{0:T(128)} %starts.1, bf16[8,12,16,2048]{3,2,1,0:T(8,128)(2,1)} %feats.1, s32[1,32]{1,0:T(1,128)} %shuf.1, bf16[8,2048]{1,0:T(8,128)(2,1)} %qf_h.1, bf16[3,2048,512]{2,1,0:T(8,128)(2,1)} %wt_h.1, ...), custom_call_target="tpu_custom_call" | custom-call | tf_op jit(solution)/shard_map/moco/pallas_call | solution.py:438
  68.2 4.9 %last.1 = (bf16[8,128]{1,0:T(8,128)(2,1)}, f32[2048,128]{1,0:T(8,128)}) custom-call(bf16[8,128]{1,0:T(8,128)(2,1)} %get-tuple-element.5.keys_ref, bf16[2048,1024]{1,0:T(8,128)(2,1)} %get-tuple-element.6.q_ref, bf16[1024,128]{1,0:T(8,128)(2,1)} %bitcast.7), custom_call_target="tpu_custom_call" | custom-call | tf_op jit(solution)/shard_map/last/pallas_call | solution.py:490

commit v4 on v3

--- a/solution.py
+++ b/solution.py
@@ -9,7 +9,7 @@
 F32, BF16, I32 = jnp.float32, jnp.bfloat16, jnp.int32
 CLIPS, FRAMES, TF, SPOTS, SIDE = 8, 8, 12, 16, 4
 C, INNER, EMB, QUEUE = 2048, 512, 128, 16384
-PLANE, LINE, PEERS, ROUNDS = 16, 8, 32, 6
+PLANE, LINE, PEERS, ROUNDS, PIECES = 16, 8, 32, 6, 4
 KC = 512
 NK = C // KC
 ROWS = CLIPS * FRAMES * SPOTS
@@ -24,10 +24,11 @@
 
 
 def kernel(
-    starts, feats, shuf, qf_h, wt_h, ws_h, we_h, g1, s1, g2, s2, g3, s3, wk_h, wq_h, queue_h,
+    starts_h, feats, shuf_h, qf_h, wt_h, ws_h, we_h, g1_h, s1_h, g2_h, s2_h, g3_h, s3_h, wk_h, wq_h, queue_h,
     keys_out, qt_out, g_out,
-    xall, xc, wt, acc, act, ws, act2, we, third, queue_v, qall, qt, wk, wq,
-    tabv, tabs, picks, sb, ra, tb, rb, qmine, gall, pooled, gvec,
+    xall, wt, acc, act, ws, act2, we, third, queue_v, qall, qt, wk, wq,
+    tabv, tabs, picks, sb, ra, tb, rb, qmine, gall, pooled, gvec, keys_v,
+    starts, shuf, g1, s1, g2, s2, g3, s3,
     hsem, asem, bsem, gsem, tsem, qsem, csem,
 ):
     i, x = lax.axis_index("dp"), lax.axis_index("bn")
@@ -51,26 +52,32 @@
         c[axis] = (c[axis] + k) % 4
         return ((c[1] * 4 + c[2]) * 2 + core, c[0])
 
-    barrier = pltpu.get_barrier_semaphore()
-    for k in range(1, PLANE):
-        pl.semaphore_signal(barrier, inc=1, device_id=plane_peer(k), device_id_type=MESH)
-    for k in range(1, LINE):
-        pl.semaphore_signal(barrier, inc=1, device_id=line_peer(k), device_id_type=MESH)
-
     def load(src, dst, n):
         return pltpu.make_async_copy(src, dst, hsem.at[n])
 
     own_q = qall.at[core, x, y, z]
     feat_loads = [load(feats.at[:, :, :, pl.ds(KC * k, KC)], xall[k], k) for k in range(NK)]
     wt_loads = [load(wt_h.at[:, pl.ds(KC * k, KC), :], wt.at[k], NK + k) for k in range(NK)]
-    small = [load(qf_h, own_q, 8), load(qf_h, qmine, 9), load(wq_h, wq, 10)]
+    small = [load(a, b, 22 + n) for n, (a, b) in enumerate(zip((g1_h, s1_h, g2_h, s2_h, g3_h, s3_h), (g1, s1, g2, s2, g3, s3)))]
+    small += [load(qf_h, own_q, 8), load(qf_h, qmine, 9), load(wq_h, wq, 10)]
     queue_load = load(queue_h, queue_v, 11)
     ws_load = load(ws_h, ws, 12)
     we_loads = [load(we_h.at[:, pl.ds(INNER * q, INNER)], we.at[q], 16 + q) for q in range(4)]
     wk_load = load(wk_h, wk, 14)
     feat_loads[0].start()
     wt_loads[0].start()
-
+    first_loads = [load(starts_h, starts, 20), load(shuf_h, shuf, 21)]
+    for d in first_loads:
+        d.start()
+    barrier = pltpu.get_barrier_semaphore()
+    for k in range(1, PLANE):
+        pl.semaphore_signal(barrier, inc=1, device_id=plane_peer(k), device_id_type=MESH)
+    for k in range(1, LINE):
+        pl.semaphore_signal(barrier, inc=1, device_id=line_peer(k), device_id_type=MESH)
+
+
+    for d in first_loads:
+        d.wait()
     row = shuf[...].astype(F32)
     sq = (PEERS, PEERS)
     r_i = lax.broadcasted_iota(I32, sq, 0)
@@ -84,23 +91,21 @@
     tabv[x, 0:1, 0:PEERS] = shuf[...]
     tabv[4, 0:1, 0:PEERS] = inverse.astype(I32)
 
-    for k in range(NK):
-        for e in (0, FRAMES + 1):
-            xc[k, :, e] = jnp.zeros((CLIPS, SPOTS, KC), BF16)
-
     def conv_one(k):
-        def pick(n, _):
-            first = starts[n]
-            for t in range(FRAMES):
-                xc[k, n, 1 + t] = xall[k][n, first + t]
-            return 0
-
-        lax.fori_loop(0, CLIPS, pick, 0)
+        empty = jnp.zeros((SPOTS, KC), BF16)
 
         def rows(p, _):
-            lhs = jnp.concatenate(
-                [xc[k, pl.ds(4 * p, 4), o : o + FRAMES].reshape(512, KC) for o in range(3)], axis=1
-            )
+            taps = []
+            for o in range(3):
+                blocks = []
+                for m in range(4):
+                    n = p * 4 + m
+                    first = starts[n] + (o - 1)
+                    for t in range(FRAMES):
+                        inside = 0 <= t + o - 1 < FRAMES
+                        blocks.append(xall[k][n, first + t] if inside else empty)
+                taps.append(jnp.concatenate(blocks, axis=0))
+            lhs = jnp.concatenate(taps, axis=1)
             r = jnp.dot(lhs, wt[k].reshape(3 * KC, INNER), preferred_element_type=F32)
             at = pl.ds(pl.multiple_of(p * 512, 512), 512)
             for q in range(4):
@@ -110,28 +115,33 @@
 
         lax.fori_loop(0, CLIPS // 4, rows, 0)
 
-    def q_region(p, done):
+    def q_region(p, phase):
         at = [pl.ds(xyz[a], 1) for a in range(3)]
-        for a in done:
-            at[a] = pl.ds(0, 4)
+        if phase >= 1:
+            at[ORDER[p][0]] = pl.ds(0, 4)
+        if phase >= 2:
+            at[ORDER[p][0]] = pl.ds(2 * (phase - 2), 2)
+            at[ORDER[p][1]] = pl.ds(0, 4)
         return qall.at[(core, *at, slice(None), pl.ds(*PARTS[p]))]
 
-    def q_send(phase):
-        for p in range(3):
-            part = q_region(p, ORDER[p][:phase])
+    def q_send(phase, parts=(0, 1, 2)):
+        for p in parts:
+            part = q_region(p, phase)
             for k in range(1, 4):
                 pltpu.make_async_remote_copy(
                     src_ref=part, dst_ref=part, send_sem=qsem.at[0, p, phase], recv_sem=qsem.at[1, p, phase],
-                    device_id=axis_peer(ORDER[p][phase], k), device_id_type=MESH,
+                    device_id=axis_peer(ORDER[p][min(phase, 2)], k), device_id_type=MESH,
                 ).start()
 
-    def q_wait(phase, side):
-        for p in range(3):
+    def q_wait(phase, side, parts=(0, 1, 2)):
+        for p in parts:
             cols = pl.ds(*PARTS[p])
+            half_phase = qall.at[0, pl.ds(0, 3), pl.ds(0, 2), :, :, cols]
             ref = (
                 qall.at[0, 0, 0, pl.ds(0, 3), :, cols],
                 qall.at[0, 0, pl.ds(0, 3), :, :, cols],
-                qall.at[0, pl.ds(0, 3), :, :, :, cols],
+                half_phase,
+                half_phase,
             )[phase]
             await_bytes(ref, qsem.at[side, p, phase])
 
@@ -198,6 +208,17 @@
             return tuple(out)
 
         return lax.fori_loop(0, ROWS // 128, body, zeros)
+
+    to_scalar = pltpu.make_async_copy(tabv, tabs, hsem.at[15])
+
+    def find_picks():
+        to_scalar.wait()
+        for k in range(LINE):
+            m = (member + k) % LINE
+            group = tabs[m // 2, 0, yz * 2 + m % 2]
+            j = tabs[4, 0, group]
+            picks[0, k] = (yz - j // 2 + PLANE - 1) % PLANE
+            picks[1, k] = jnp.where(j % 2 == core, 1, 0).astype(I32)
 
     for k in range(NK):
         feat_loads[k].wait()
@@ -229,19 +250,12 @@
         if k == 2:
             q_wait(0, 1)
             q_send(1)
+            await_bytes(tabv.at[pl.ds(0, 3)], tsem.at[1])
+            to_scalar.start()
+        if k == 3:
+            find_picks()
     put_stats(0, total_of(acc))
     plane_send(0)
-
-    await_bytes(tabv.at[pl.ds(0, 3)], tsem.at[1])
-    to_scalar = pltpu.make_async_copy(tabv, tabs, hsem.at[15])
-    to_scalar.start()
-    to_scalar.wait()
-    for k in range(LINE):
-        m = (member + k) % LINE
-        group = tabs[m // 2, 0, yz * 2 + m % 2]
-        j = tabs[4, 0, group]
-        picks[0, k] = (yz - j // 2 + PLANE - 1) % PLANE
-        picks[1, k] = jnp.where(j % 2 == core, 1, 0).astype(I32)
 
     zq = jnp.dot(qmine[...], wq[...], preferred_element_type=F32)
     length = jnp.sqrt(jnp.sum(zq * zq, axis=-1, keepdims=True) + TINY)
@@ -264,12 +278,15 @@
         return lax.fori_loop(lo, hi, body, carry)
 
     carry = (jnp.zeros((CLIPS, 1), F32), jnp.zeros((CLIPS, EMB), F32))
-    carry = queue_part(0, 8, carry)
+    carry = queue_part(0, 6, carry)
 
     plane_forward(0)
+    q_wait(1, 1)
+    q_send(2, (1, 2))
+    carry = queue_part(6, 9, carry)
     tile = line_finish(0)
-    q_wait(1, 1)
-    q_send(2)
+    q_send(2, (0,))
+    q_send(3, (1, 2))
 
     scale, shift = affine(tile, g1[...], s1[...])
     for r in range(4):
@@ -312,41 +329,51 @@
     lax.fori_loop(0, 2, middle, 0)
     put_stats(1, total_of(acc))
     plane_send(1)
-    carry = queue_part(8, 16, carry)
+    q_send(3, (0,))
+    carry = queue_part(9, 15, carry)
     plane_forward(1)
+    carry = queue_part(15, 16, carry)
     tile = line_finish(1)
+    q_wait(2, 1)
+    q_wait(3, 1)
+    core_copy.start()
 
     scale, shift = affine(tile, g2[...], s2[...])
 
+    side = (128, 128)
+    to = lax.broadcasted_iota(I32, side, 0)
+    source = lax.broadcasted_iota(I32, side, 1)
+    swap = jnp.where((to % 16) * 8 + to // 16 == source, 1.0, 0.0).astype(BF16)
+
     def norm_two(p, _):
-        for h in range(8):
-            v = rows_of(acc, pl.ds(p * 8 + h, SPOTS, stride=64))
-            act2[pl.ds(pl.multiple_of(p * 128, 128) + h * 16, 16), :] = jnp.maximum(
-                v * scale + shift, 0.0
-            ).astype(BF16)
+        for n in (2 * p, 2 * p + 1):
+            chunks = []
+            for q in range(4):
+                lanes = slice(128 * q, 128 * (q + 1))
+                rows = [acc[q, pl.ds(pl.multiple_of(n * 8, 8) + 64 * s, 8), :] for s in range(SPOTS)]
+                v = jnp.concatenate(rows, axis=0) * scale[:, lanes] + shift[:, lanes]
+                chunks.append(jnp.maximum(v, 0.0).astype(BF16))
+            v = jnp.dot(swap, jnp.concatenate(chunks, axis=1), preferred_element_type=F32)
+            act2[pl.ds(pl.multiple_of(n * 128, 128), 128), :] = v.astype(BF16)
         return 0
 
-    lax.fori_loop(0, CLIPS, norm_two, 0)
+    lax.fori_loop(0, CLIPS // 2, norm_two, 0)
     for d in we_loads:
         d.wait()
 
     for q in range(4):
 
-        def expand(p, carry):
-            at = pl.ds(pl.multiple_of(p * 512, 512), 512)
+        sums = list(zeros)
+        for p in range(2):
+            at = pl.ds(p * 512, 512)
             v = jnp.dot(act2[at, :], we[q], preferred_element_type=F32)
             third[q, at, :] = v
-            out = list(carry)
             for c in range(4):
                 a, b = sums_of(v[:, 128 * c : 128 * (c + 1)])
-                out[2 * c] = out[2 * c] + a
-                out[2 * c + 1] = out[2 * c + 1] + b
-            return tuple(out)
-
-        put_stats(2 + q, lax.fori_loop(0, 2, expand, zeros))
+                sums[2 * c] = sums[2 * c] + a
+                sums[2 * c + 1] = sums[2 * c + 1] + b
+        put_stats(2 + q, sums)
         plane_send(2 + q)
-    q_wait(2, 1)
-    core_copy.start()
     for q in range(4):
         plane_forward(2 + q)
 
@@ -356,9 +383,10 @@
 
         def pool(n, _):
             at = pl.ds(pl.multiple_of(n * 128, 128), 128)
+            first = starts[n]
             for c in range(4):
                 lanes = slice(128 * c, 128 * (c + 1))
-                kept = xc[q, n, 1 : 1 + FRAMES, :, lanes].reshape(128, 128).astype(F32)
+                kept = jnp.concatenate([xall[q][n, first + t, :, lanes] for t in range(FRAMES)], axis=0).astype(F32)
                 v = jnp.maximum(third[q, at, lanes] * scale[:, lanes] + shift[:, lanes] + kept, 0.0)
                 pooled[n, :, INNER * q + 128 * c : INNER * q + 128 * (c + 1)] = jnp.sum(
                     v.reshape(16, 8, 128), axis=0
@@ -371,7 +399,9 @@
     projected = jnp.dot(mean.astype(BF16), wk[...], preferred_element_type=F32)
     norm = jnp.sum(projected * projected, axis=-1, keepdims=True) + TINY
     keys = (projected * lax.rsqrt(norm)).astype(BF16)
-    keys_out[...] = keys
+    keys_v[...] = keys
+    keys_store = load(keys_v, keys_out, 12)
+    keys_store.start()
 
     held = keys.astype(F32)
     total, mix = carry
@@ -408,9 +438,10 @@
     await_bytes(gall_line, gsem.at[3])
     own_half.wait()
     qt_store.wait()
+    keys_store.wait()
 
     await_bytes(tabv.at[pl.ds(0, 3)], tsem.at[0])
-    for phase in range(3):
+    for phase in range(4):
         q_wait(phase, 0)
     core_copy.wait_send()
     for r in range(ROUNDS):
@@ -420,17 +451,39 @@
     await_bytes(gall_line, gsem.at[2])
 
 
-def last(keys_ref, q_ref, g_ref, keys_out, grad_out):
-    keys_out[...] = keys_ref[...]
-    grad_out[...] = jnp.dot(q_ref[...], g_ref[...], preferred_element_type=F32)
+def last(keys_ref, q_ref, g_ref, keys_out, grad_out, keys_v, q_v, g_v, out_v, sem):
+    tall = C // PIECES
+
+    def rows(n):
+        return pl.ds(n * tall, tall)
+
+    keys_in = pltpu.make_async_copy(keys_ref, keys_v, sem.at[0])
+    g_in = pltpu.make_async_copy(g_ref, g_v, sem.at[1])
+    q_in = [pltpu.make_async_copy(q_ref.at[rows(n)], q_v.at[n], sem.at[2 + n]) for n in range(PIECES)]
+    g_in.start()
+    for d in q_in:
+        d.start()
+    keys_in.start()
+    stores = []
+    g_in.wait()
+    for n in range(PIECES):
+        q_in[n].wait()
+        out_v[n] = jnp.dot(q_v[n], g_v[...], preferred_element_type=F32)
+        d = pltpu.make_async_copy(out_v.at[n], grad_out.at[rows(n)], sem.at[2 + PIECES + n])
+        d.start()
+        stores.append(d)
+    keys_in.wait()
+    d = pltpu.make_async_copy(keys_v, keys_out, sem.at[0])
+    d.start()
+    for e in stores:
+        e.wait()
+    d.wait()
 
 
 def local(
     key_feats, clip_starts, shuffle, query_feats, conv_time, conv_space, conv_expand,
     gain_one, shift_one, gain_two, shift_two, gain_three, shift_three, w_key, w_query, queue,
 ):
-    vmem = pl.BlockSpec(memory_space=pltpu.VMEM)
-    smem = pl.BlockSpec(memory_space=pltpu.SMEM)
     hbm = pl.BlockSpec(memory_space=pltpu.HBM)
     V = pltpu.VMEM
     DMA = pltpu.SemaphoreType.DMA
@@ -443,11 +496,10 @@
             jax.ShapeDtypeStruct((C, 1024), BF16),
             jax.ShapeDtypeStruct((LINE, PLANE, CLIPS, EMB), BF16),
         ),
-        in_specs=[smem, hbm, vmem, hbm, hbm, hbm, hbm] + [vmem] * 6 + [hbm] * 3,
-        out_specs=(vmem, hbm, hbm),
+        in_specs=[hbm] * 16,
+        out_specs=(hbm, hbm, hbm),
         scratch_shapes=[
             [V((CLIPS, TF, SPOTS, KC), BF16) for _ in range(NK)],
-            V((NK, CLIPS, FRAMES + 2, SPOTS, KC), BF16),
             V((NK, 3, KC, INNER), BF16),
             V((4, ROWS, 128), F32),
             V((SIDE, SIDE + 2, 64, INNER), BF16),
@@ -471,12 +523,16 @@
             V((LINE, PLANE, CLIPS, EMB), BF16),
             V((CLIPS, 8, C), F32),
             V((CLIPS, EMB), BF16),
-            DMA((20,)),
+            V((CLIPS, EMB), BF16),
+            pltpu.SMEM((CLIPS,), I32),
+            V((1, PEERS), I32),
+            *[V((1, n), F32) for n in (INNER,) * 4 + (C,) * 2],
+            DMA((30,)),
             DMA((2, ROUNDS)),
             DMA((2, ROUNDS)),
             DMA((4,)),
             DMA((2,)),
-            DMA((2, 3, 3)),
+            DMA((2, 3, 4)),
             DMA((2,)),
         ],
         compiler_params=pltpu.CompilerParams(
@@ -486,18 +542,19 @@
         clip_starts, key_feats, shuffle, query_feats, conv_time, conv_space, conv_expand,
         *rows, w_key, w_query, queue,
     )
-    tall = C // 4
     return pl.pallas_call(
         last,
         name="last",
-        grid=(4,),
         out_shape=(jax.ShapeDtypeStruct((CLIPS, EMB), BF16), jax.ShapeDtypeStruct((C, EMB), F32)),
-        in_specs=[
-            pl.BlockSpec((CLIPS, EMB), lambda n: (0, 0)),
-            pl.BlockSpec((tall, 1024), lambda n: (n, 0)),
-            pl.BlockSpec((1024, EMB), lambda n: (0, 0)),
+        in_specs=[hbm] * 3,
+        out_specs=(hbm, hbm),
+        scratch_shapes=[
+            V((CLIPS, EMB), BF16),
+            V((PIECES, C // PIECES, 1024), BF16),
+            V((1024, EMB), BF16),
+            V((PIECES, C // PIECES, EMB), F32),
+            DMA((2 + 2 * PIECES,)),
         ],
-        out_specs=(pl.BlockSpec((CLIPS, EMB), lambda n: (0, 0)), pl.BlockSpec((tall, EMB), lambda n: (n, 0))),
     )(keys, q_t, grads.reshape(1024, EMB))
 
 

time: 73.3 us -> 66.9 us (0.913)
  Pallas kernels: 72.4 us -> 66.2 us
    pallas_call x1, Pallas kernels: 67.6 us -> 61.3 us  [local(): pl.pallas_call(kernel, name='moco', out_shape=(jax.ShapeDtypeStruct((CLIP...]
where the time goes in v4:
time: 66.9 us; the launch traced here: 66.8 us
  Pallas kernels  66.2 us (99%)
    pallas_call x1, Pallas kernels, local(): pl.pallas_call(kernel, name='moco', out_shape=(jax.ShapeDtypeStruct((CLIP...  61.3 us
    pallas_call x1, Pallas kernels, local(): pl.pallas_call(last, name='last', out_shape=(jax.ShapeDtypeStruct((CLIPS,...  4.86 us

profile of v4, /device:TPU:1, one launch (start us, length us, event | category | flops | bytes accessed | tf_op | source)
XLA Modules:
  0.0 66.8 jit_solution(11644860060718076339)
XLA Ops:
  0.6 61.3 %moco.1 = (bf16[8,128]{1,0:T(8,128)(2,1)}, bf16[2048,1024]{1,0:T(8,128)(2,1)}, bf16[8,16,8,128]{3,2,1,0:T(8,128)(2,1)}) custom-call(s32[8]{0:T(128)} %starts_h.1, bf16[8,12,16,2048]{3,2,1,0:T(8,128)(2,1)} %feats.1, s32[1,32]{1,0:T(1,128)} %shuf_h.1, bf16[8,2048]{1,0:T(8,128)(2,1)} %qf_h.1, bf16[3,2048,512]{2,1,0:T(8,128)(2,1)} %wt_h.1, ...), custom_call_target="tpu_custom_call" | custom-call | tf_op jit(solution)/shard_map/moco/pallas_call | solution.py:491
  62.0 4.9 %last.1 = (bf16[8,128]{1,0:T(8,128)(2,1)}, f32[2048,128]{1,0:T(8,128)}) custom-call(bf16[8,128]{1,0:T(8,128)(2,1)} %get-tuple-element.5.keys_ref, bf16[2048,1024]{1,0:T(8,128)(2,1)} %get-tuple-element.6.q_ref, bf16[1024,128]{1,0:T(8,128)(2,1)} %bitcast.7), custom_call_target="tpu_custom_call" | custom-call | tf_op jit(solution)/shard_map/last/pallas_call | solution.py:545

commit v5 on v4

--- a/solution.py
+++ b/solution.py
@@ -7,9 +7,9 @@
 
 MESH = pl.DeviceIdType.MESH
 F32, BF16, I32 = jnp.float32, jnp.bfloat16, jnp.int32
-CLIPS, FRAMES, TF, SPOTS, SIDE = 8, 8, 12, 16, 4
+CLIPS, FRAMES, TF, SPOTS, SIDE, CHIPS = 8, 8, 12, 16, 4, 64
 C, INNER, EMB, QUEUE = 2048, 512, 128, 16384
-PLANE, LINE, PEERS, ROUNDS, PIECES = 16, 8, 32, 6, 4
+PLANE, LINE, PEERS, ROUNDS, PIECES = 16, 8, 32, 7, 8
 KC = 512
 NK = C // KC
 ROWS = CLIPS * FRAMES * SPOTS
@@ -26,7 +26,7 @@
 def kernel(
     starts_h, feats, shuf_h, qf_h, wt_h, ws_h, we_h, g1_h, s1_h, g2_h, s2_h, g3_h, s3_h, wk_h, wq_h, queue_h,
     keys_out, qt_out, g_out,
-    xall, wt, acc, act, ws, act2, we, third, queue_v, qall, qt, wk, wq,
+    xall, wt, acc, second, act, ws, act2, we, third, queue_v, qall, qt, wk, wq,
     tabv, tabs, picks, sb, ra, tb, rb, qmine, gall, pooled, gvec, keys_v,
     starts, shuf, g1, s1, g2, s2, g3, s3,
     hsem, asem, bsem, gsem, tsem, qsem, csem,
@@ -36,9 +36,7 @@
     y, z = yz // 4, yz % 4
     xyz = (x, y, z)
     member = x * 2 + core
-    half = core * 4 + x
-    gall_plane = gall.at[0, pl.ds(0, PLANE - 1)]
-    gall_line = gall.at[pl.ds(0, LINE - 1)]
+    chip = x * 16 + yz
 
     def plane_peer(k):
         return ((yz + k) % PLANE * 2 + core, x)
@@ -46,6 +44,13 @@
     def line_peer(k):
         m = (member + k) % LINE
         return (yz * 2 + m % 2, m // 2)
+
+    def chip_peer(k):
+        c = (x + k // 16) % 4, (y + k // 4 % 4) % 4, (z + k % 4) % 4
+        return ((c[1] * 4 + c[2]) * 2 + core, c[0])
+
+    def cross_peer(k):
+        return (yz * 2 + 1 - core, (x + k) % 4)
 
     def axis_peer(axis, k):
         c = list(xyz)
@@ -57,7 +62,10 @@
 
     own_q = qall.at[core, x, y, z]
     feat_loads = [load(feats.at[:, :, :, pl.ds(KC * k, KC)], xall[k], k) for k in range(NK)]
-    wt_loads = [load(wt_h.at[:, pl.ds(KC * k, KC), :], wt.at[k], NK + k) for k in range(NK)]
+    wt_loads = [
+        [load(wt_h.at[:, pl.ds(KC * k, KC), pl.ds(256 * h, 256)], wt.at[h, k], (4, 30)[h] + k) for k in range(NK)]
+        for h in range(2)
+    ]
     small = [load(a, b, 22 + n) for n, (a, b) in enumerate(zip((g1_h, s1_h, g2_h, s2_h, g3_h, s3_h), (g1, s1, g2, s2, g3, s3)))]
     small += [load(qf_h, own_q, 8), load(qf_h, qmine, 9), load(wq_h, wq, 10)]
     queue_load = load(queue_h, queue_v, 11)
@@ -65,15 +73,15 @@
     we_loads = [load(we_h.at[:, pl.ds(INNER * q, INNER)], we.at[q], 16 + q) for q in range(4)]
     wk_load = load(wk_h, wk, 14)
     feat_loads[0].start()
-    wt_loads[0].start()
+    wt_loads[0][0].start()
     first_loads = [load(starts_h, starts, 20), load(shuf_h, shuf, 21)]
     for d in first_loads:
         d.start()
     barrier = pltpu.get_barrier_semaphore()
-    for k in range(1, PLANE):
-        pl.semaphore_signal(barrier, inc=1, device_id=plane_peer(k), device_id_type=MESH)
-    for k in range(1, LINE):
-        pl.semaphore_signal(barrier, inc=1, device_id=line_peer(k), device_id_type=MESH)
+    for k in range(1, CHIPS):
+        pl.semaphore_signal(barrier, inc=1, device_id=chip_peer(k), device_id_type=MESH)
+    for k in range(4):
+        pl.semaphore_signal(barrier, inc=1, device_id=cross_peer(k), device_id_type=MESH)
 
 
     for d in first_loads:
@@ -91,7 +99,7 @@
     tabv[x, 0:1, 0:PEERS] = shuf[...]
     tabv[4, 0:1, 0:PEERS] = inverse.astype(I32)
 
-    def conv_one(k):
+    def conv_one(k, h):
         empty = jnp.zeros((SPOTS, KC), BF16)
 
         def rows(p, _):
@@ -106,10 +114,12 @@
                         blocks.append(xall[k][n, first + t] if inside else empty)
                 taps.append(jnp.concatenate(blocks, axis=0))
             lhs = jnp.concatenate(taps, axis=1)
-            r = jnp.dot(lhs, wt[k].reshape(3 * KC, INNER), preferred_element_type=F32)
+            w = wt[h, k].reshape(3 * KC, 256)
+            r = jnp.dot(lhs, w, preferred_element_type=F32)
             at = pl.ds(pl.multiple_of(p * 512, 512), 512)
-            for q in range(4):
-                v = r[:, 128 * q : 128 * (q + 1)]
+            for c in range(2):
+                q = 2 * h + c
+                v = r[:, 128 * c : 128 * (c + 1)]
                 acc[q, at, :] = v if k == 0 else acc[q, at, :] + v
             return 0
 
@@ -174,14 +184,16 @@
             mine = mine + rb[r, k]
         return mine
 
-    def put_stats(r, parts):
-        for q in range(4):
-            sb[r, q : q + 1, :] = jnp.sum(parts[2 * q], axis=0, keepdims=True)
-            sb[r, 4 + q : 5 + q, :] = jnp.sum(parts[2 * q + 1], axis=0, keepdims=True)
-
-    def affine(tile, gain, shift):
+    def put_stats(r, parts, chunks=(0, 1, 2, 3)):
+        if len(chunks) < 4:
+            sb[r] = jnp.zeros((8, 128), F32)
+        for n, q in enumerate(chunks):
+            sb[r, q : q + 1, :] = jnp.sum(parts[2 * n], axis=0, keepdims=True)
+            sb[r, 4 + q : 5 + q, :] = jnp.sum(parts[2 * n + 1], axis=0, keepdims=True)
+
+    def affine(tile, gain, shift, chunks=(0, 1, 2, 3)):
         scales, shifts = [], []
-        for q in range(4):
+        for q in chunks:
             m = tile[q : q + 1, :] * (1.0 / COUNT)
             w = tile[4 + q : 5 + q, :] * (1.0 / COUNT) - m * m
             scale = gain[:, 128 * q : 128 * (q + 1)] * lax.rsqrt(w + EPS)
@@ -195,19 +207,19 @@
         v = block.reshape(-1, 8, 128)
         return jnp.sum(v, axis=0), jnp.sum(v * v, axis=0)
 
-    def rows_of(ref, at):
-        return jnp.concatenate([ref[q, at, :] for q in range(4)], axis=1)
-
-    def total_of(ref):
+    def rows_of(ref, at, chunks=(0, 1, 2, 3)):
+        return jnp.concatenate([ref[q, at, :] for q in chunks], axis=1)
+
+    def total_of(ref, chunks=(0, 1, 2, 3)):
         def body(p, carry):
             out = list(carry)
-            for q in range(4):
+            for n, q in enumerate(chunks):
                 a, b = sums_of(ref[q, pl.ds(pl.multiple_of(p * 128, 128), 128), :])
-                out[2 * q] = out[2 * q] + a
-                out[2 * q + 1] = out[2 * q + 1] + b
+                out[2 * n] = out[2 * n] + a
+                out[2 * n + 1] = out[2 * n + 1] + b
             return tuple(out)
 
-        return lax.fori_loop(0, ROWS // 128, body, zeros)
+        return lax.fori_loop(0, ROWS // 128, body, zeros[: 2 * len(chunks)])
 
     to_scalar = pltpu.make_async_copy(tabv, tabs, hsem.at[15])
 
@@ -222,23 +234,25 @@
 
     for k in range(NK):
         feat_loads[k].wait()
-        wt_loads[k].wait()
+        wt_loads[0][k].wait()
+        for ahead in {0: (1, 2), 1: (3,)}.get(k, ()):
+            feat_loads[ahead].start()
+            wt_loads[0][ahead].start()
         if k == 0:
             for d in small:
                 d.start()
-        if k + 1 < NK:
-            feat_loads[k + 1].start()
-            wt_loads[k + 1].start()
         if k == 2:
+            for d in wt_loads[1]:
+                d.start()
             queue_load.start()
+        if k == 3:
             ws_load.start()
-        if k == 3:
             for d in we_loads:
                 d.start()
             wk_load.start()
-        conv_one(k)
-        if k == 0:
-            pl.semaphore_wait(barrier, PLANE - 1 + LINE - 1)
+        conv_one(k, 0)
+        if k == 2:
+            pl.semaphore_wait(barrier, CHIPS - 1 + 4)
             for d in small:
                 d.wait()
             for n in range(1, 4):
@@ -247,20 +261,26 @@
                     device_id=axis_peer(0, n), device_id_type=MESH,
                 ).start()
             q_send(0)
-        if k == 2:
+    put_stats(0, total_of(acc, (0, 1)), (0, 1))
+    plane_send(0)
+    for k in range(NK):
+        wt_loads[1][k].wait()
+        conv_one(k, 1)
+        if k == 1:
             q_wait(0, 1)
             q_send(1)
             await_bytes(tabv.at[pl.ds(0, 3)], tsem.at[1])
             to_scalar.start()
-        if k == 3:
+        if k == 2:
             find_picks()
-    put_stats(0, total_of(acc))
-    plane_send(0)
+    put_stats(6, total_of(acc, (2, 3)), (2, 3))
+    plane_send(6)
 
     zq = jnp.dot(qmine[...], wq[...], preferred_element_type=F32)
     length = jnp.sqrt(jnp.sum(zq * zq, axis=-1, keepdims=True) + TINY)
     unit = zq / length
     unit_b = unit.astype(BF16)
+    plane_forward(0)
     queue_load.wait()
 
     def queue_part(lo, hi, carry):
@@ -278,59 +298,73 @@
         return lax.fori_loop(lo, hi, body, carry)
 
     carry = (jnp.zeros((CLIPS, 1), F32), jnp.zeros((CLIPS, EMB), F32))
-    carry = queue_part(0, 6, carry)
-
-    plane_forward(0)
-    q_wait(1, 1)
-    q_send(2, (1, 2))
-    carry = queue_part(6, 9, carry)
-    tile = line_finish(0)
-    q_send(2, (0,))
-    q_send(3, (1, 2))
-
-    scale, shift = affine(tile, g1[...], s1[...])
     for r in range(4):
         for e in (0, SIDE + 1):
             act[r, e] = jnp.zeros((64, INNER), BF16)
 
-    def norm_one(p, _):
-        for r in range(SIDE):
-            for c in range(SIDE):
-                both = [
-                    rows_of(acc, pl.ds((2 * p + h) * 128 + SIDE * r + c, FRAMES, stride=SPOTS)) for h in range(2)
-                ]
-                v = jnp.concatenate(both, axis=0)
-                v = jnp.maximum(v * scale + shift, 0.0).astype(BF16)
-                act[r, c + 1, pl.ds(pl.multiple_of(p * 16, 16), 16), :] = v
-        return 0
-
-    lax.fori_loop(0, CLIPS // 2, norm_one, 0)
-
+    def normalize_one(h, tile):
+        chunks = (2 * h, 2 * h + 1)
+        scale, shift = affine(tile, g1[...], s1[...], chunks)
+
+        def norm_one(p, _):
+            for r in range(SIDE):
+                for c in range(SIDE):
+                    both = [
+                        rows_of(acc, pl.ds((2 * p + m) * 128 + SIDE * r + c, FRAMES, stride=SPOTS), chunks)
+                        for m in range(2)
+                    ]
+                    v = jnp.concatenate(both, axis=0)
+                    v = jnp.maximum(v * scale + shift, 0.0).astype(BF16)
+                    act[r, c + 1, pl.ds(pl.multiple_of(p * 16, 16), 16), 256 * h : 256 * (h + 1)] = v
+            return 0
+
+        lax.fori_loop(0, CLIPS // 2, norm_one, 0)
+
+    def row_conv(h, r, base, tap, taps):
+        lanes = slice(256 * h, 256 * (h + 1))
+        lhs = jnp.concatenate(
+            [act[base + d, c : c + SIDE, :, lanes].reshape(256, 256) for d in range(taps) for c in range(3)], axis=1
+        )
+        w = ws[pl.ds(tap, 3 * taps), lanes].reshape(3 * taps * 256, INNER)
+        v = jnp.dot(lhs, w, preferred_element_type=F32)
+        at = pl.ds(pl.multiple_of(r * 256, 256), 256)
+        for q in range(4):
+            part = v[:, 128 * q : 128 * (q + 1)]
+            second[q, at, :] = part if h == 0 else second[q, at, :] + part
+
+    def edges(h):
+        def edge(n, _):
+            row_conv(h, 3 * n, 2 * n, 3 - 3 * n, 2)
+            return 0
+
+        lax.fori_loop(0, 2, edge, 0)
+
+    def middles(h):
+        def middle(n, _):
+            row_conv(h, 1 + n, n, 0, 3)
+            return 0
+
+        lax.fori_loop(0, 2, middle, 0)
+
+    carry = queue_part(0, 7, carry)
+    plane_forward(6)
+    q_wait(1, 1)
+    q_send(2, (1, 2))
+    tile = line_finish(0)
+    normalize_one(0, tile)
     ws_load.wait()
-
-    def row_conv(r, base, tap, taps):
-        lhs = jnp.concatenate(
-            [act[base + d, c : c + SIDE].reshape(256, INNER) for d in range(taps) for c in range(3)], axis=1
-        )
-        w = ws[pl.ds(tap, 3 * taps)].reshape(3 * taps * INNER, INNER)
-        v = jnp.dot(lhs, w, preferred_element_type=F32)
-        for q in range(4):
-            acc[q, pl.ds(pl.multiple_of(r * 256, 256), 256), :] = v[:, 128 * q : 128 * (q + 1)]
-
-    def edge(n, _):
-        row_conv(3 * n, 2 * n, 3 - 3 * n, 2)
-        return 0
-
-    def middle(n, _):
-        row_conv(1 + n, n, 0, 3)
-        return 0
-
-    lax.fori_loop(0, 2, edge, 0)
-    lax.fori_loop(0, 2, middle, 0)
-    put_stats(1, total_of(acc))
+    edges(0)
+    middles(0)
+    tile = line_finish(6)
+    q_send(2, (0,))
+    q_send(3, (1, 2))
+    normalize_one(1, tile)
+    edges(1)
+    middles(1)
+    put_stats(1, total_of(second))
     plane_send(1)
     q_send(3, (0,))
-    carry = queue_part(9, 15, carry)
+    carry = queue_part(7, 15, carry)
     plane_forward(1)
     carry = queue_part(15, 16, carry)
     tile = line_finish(1)
@@ -350,7 +384,7 @@
             chunks = []
             for q in range(4):
                 lanes = slice(128 * q, 128 * (q + 1))
-                rows = [acc[q, pl.ds(pl.multiple_of(n * 8, 8) + 64 * s, 8), :] for s in range(SPOTS)]
+                rows = [second[q, pl.ds(pl.multiple_of(n * 8, 8) + 64 * s, 8), :] for s in range(SPOTS)]
                 v = jnp.concatenate(rows, axis=0) * scale[:, lanes] + shift[:, lanes]
                 chunks.append(jnp.maximum(v, 0.0).astype(BF16))
             v = jnp.dot(swap, jnp.concatenate(chunks, axis=1), preferred_element_type=F32)
@@ -362,7 +396,6 @@
         d.wait()
 
     for q in range(4):
-
         sums = list(zeros)
         for p in range(2):
             at = pl.ds(p * 512, 512)
@@ -410,12 +443,12 @@
     grad = (mix / whole + (e_pos / whole - 1.0) * held) * 5.0
     radial = jnp.sum(unit * grad, axis=-1, keepdims=True)
     gvec[...] = ((grad - radial * unit) / length).astype(BF16)
-    for k in range(1, PLANE):
+    for k in range(1, CHIPS):
         pltpu.make_async_remote_copy(
-            src_ref=gvec, dst_ref=gall.at[half, yz], send_sem=gsem.at[0], recv_sem=gsem.at[1],
-            device_id=plane_peer(k), device_id_type=MESH,
+            src_ref=gvec, dst_ref=gall.at[chip], send_sem=gsem.at[0], recv_sem=gsem.at[1],
+            device_id=chip_peer(k), device_id_type=MESH,
         ).start()
-    gall[half, yz] = gvec[...]
+    gall[chip] = gvec[...]
     core_copy.wait_recv()
 
     def turn(n, _):
@@ -427,15 +460,15 @@
     lax.fori_loop(0, C // 128, turn, 0)
     qt_store = load(qt, qt_out, 15)
     qt_store.start()
-    await_bytes(gall_plane, gsem.at[1])
-    own_half = pltpu.make_async_copy(gall.at[half], g_out.at[half], hsem.at[13])
+    await_bytes(gall.at[pl.ds(0, CHIPS - 1)], gsem.at[1])
+    own_half = pltpu.make_async_copy(gall, g_out.at[core], hsem.at[13])
     own_half.start()
-    for k in range(1, LINE):
-        pltpu.make_async_remote_copy(
-            src_ref=gall.at[half], dst_ref=g_out.at[half], send_sem=gsem.at[2], recv_sem=gsem.at[3],
-            device_id=line_peer(k), device_id_type=MESH,
-        ).start()
-    await_bytes(gall_line, gsem.at[3])
+    grads_copy = pltpu.make_async_remote_copy(
+        src_ref=gall, dst_ref=g_out.at[core], send_sem=gsem.at[2], recv_sem=gsem.at[3],
+        device_id=cross_peer(0), device_id_type=MESH,
+    )
+    grads_copy.start()
+    grads_copy.wait_recv()
     own_half.wait()
     qt_store.wait()
     keys_store.wait()
@@ -447,8 +480,8 @@
     for r in range(ROUNDS):
         await_bytes(ra[r].at[pl.ds(0, PLANE - 1)], asem.at[0, r])
         await_bytes(rb.at[r, pl.ds(0, LINE - 1)], bsem.at[0, r])
-    await_bytes(gall_plane, gsem.at[0])
-    await_bytes(gall_line, gsem.at[2])
+    await_bytes(gall.at[pl.ds(0, CHIPS - 1)], gsem.at[0])
+    grads_copy.wait_send()
 
 
 def last(keys_ref, q_ref, g_ref, keys_out, grad_out, keys_v, q_v, g_v, out_v, sem):
@@ -494,13 +527,14 @@
         out_shape=(
             jax.ShapeDtypeStruct((CLIPS, EMB), BF16),
             jax.ShapeDtypeStruct((C, 1024), BF16),
-            jax.ShapeDtypeStruct((LINE, PLANE, CLIPS, EMB), BF16),
+            jax.ShapeDtypeStruct((2, CHIPS, CLIPS, EMB), BF16),
         ),
         in_specs=[hbm] * 16,
         out_specs=(hbm, hbm, hbm),
         scratch_shapes=[
             [V((CLIPS, TF, SPOTS, KC), BF16) for _ in range(NK)],
-            V((NK, 3, KC, INNER), BF16),
+            V((2, NK, 3, KC, 256), BF16),
+            V((4, ROWS, 128), F32),
             V((4, ROWS, 128), F32),
             V((SIDE, SIDE + 2, 64, INNER), BF16),
             V((9, INNER, INNER), BF16),
@@ -520,14 +554,14 @@
             V((ROUNDS, LINE - 1, 8, 128), F32),
             V((ROUNDS, LINE - 1, 8, 128), F32),
             V((CLIPS, C), BF16),
-            V((LINE, PLANE, CLIPS, EMB), BF16),
+            V((CHIPS, CLIPS, EMB), BF16),
             V((CLIPS, 8, C), F32),
             V((CLIPS, EMB), BF16),
             V((CLIPS, EMB), BF16),
             pltpu.SMEM((CLIPS,), I32),
             V((1, PEERS), I32),
             *[V((1, n), F32) for n in (INNER,) * 4 + (C,) * 2],
-            DMA((30,)),
+            DMA((34,)),
             DMA((2, ROUNDS)),
             DMA((2, ROUNDS)),
             DMA((4,)),

time: 66.9 us -> 65.7 us (0.982)
  Pallas kernels: 66.2 us -> 64.9 us
where the time goes in v5:
time: 65.7 us; the launch traced here: 65.5 us
  Pallas kernels  64.9 us (99%)
    pallas_call x1, Pallas kernels, local(): pl.pallas_call(kernel, name='moco', out_shape=(jax.ShapeDtypeStruct((CLIP...  60.7 us
    pallas_call x1, Pallas kernels, local(): pl.pallas_call(last, name='last', out_shape=(jax.ShapeDtypeStruct((CLIPS,...  4.24 us

profile of v5, /device:TPU:1, one launch (start us, length us, event | category | flops | bytes accessed | tf_op | source)
XLA Modules:
  0.0 65.5 jit_solution(636040408704572592)
XLA Ops:
  0.6 60.7 %moco.1 = (bf16[8,128]{1,0:T(8,128)(2,1)}, bf16[2048,1024]{1,0:T(8,128)(2,1)}, bf16[2,64,8,128]{3,2,1,0:T(8,128)(2,1)}) custom-call(s32[8]{0:T(128)} %starts_h.1, bf16[8,12,16,2048]{3,2,1,0:T(8,128)(2,1)} %feats.1, s32[1,32]{1,0:T(1,128)} %shuf_h.1, bf16[8,2048]{1,0:T(8,128)(2,1)} %qf_h.1, bf16[3,2048,512]{2,1,0:T(8,128)(2,1)} %wt_h.1, ...), custom_call_target="tpu_custom_call" | custom-call | tf_op jit(solution)/shard_map/moco/pallas_call | solution.py:524
  61.3 4.2 %last.1 = (bf16[8,128]{1,0:T(8,128)(2,1)}, f32[2048,128]{1,0:T(8,128)}) custom-call(bf16[8,128]{1,0:T(8,128)(2,1)} %get-tuple-element.5.keys_ref, bf16[2048,1024]{1,0:T(8,128)(2,1)} %get-tuple-element.6.q_ref, bf16[1024,128]{1,0:T(8,128)(2,1)} %bitcast.7), custom_call_target="tpu_custom_call" | custom-call | tf_op jit(solution)/shard_map/last/pallas_call | solution.py:579

commit v6 on v5

--- a/solution.py
+++ b/solution.py
@@ -49,6 +49,9 @@
         c = (x + k // 16) % 4, (y + k // 4 % 4) % 4, (z + k % 4) % 4
         return ((c[1] * 4 + c[2]) * 2 + core, c[0])
 
+    def hops(k):
+        return sum(min(d, 4 - d) for d in (k // 16, k // 4 % 4, k % 4))
+
     def cross_peer(k):
         return (yz * 2 + 1 - core, (x + k) % 4)
 
@@ -61,9 +64,33 @@
         return pltpu.make_async_copy(src, dst, hsem.at[n])
 
     own_q = qall.at[core, x, y, z]
-    feat_loads = [load(feats.at[:, :, :, pl.ds(KC * k, KC)], xall[k], k) for k in range(NK)]
+    class Pieces:
+        def __init__(self, pairs, whole, n):
+            self.copies = [load(src, dst, n) for src, dst in pairs]
+            self.whole, self.n = whole, n
+
+        def start(self):
+            for d in self.copies:
+                d.start()
+
+        def wait(self):
+            await_bytes(self.whole, hsem.at[self.n])
+
+    feat_loads = [
+        Pieces(
+            [(feats.at[pl.ds(2 * m, 2), :, :, pl.ds(KC * k, KC)], xall[k].at[pl.ds(2 * m, 2)]) for m in range(4)],
+            xall[k], k,
+        )
+        for k in range(NK)
+    ]
     wt_loads = [
-        [load(wt_h.at[:, pl.ds(KC * k, KC), pl.ds(256 * h, 256)], wt.at[h, k], (4, 30)[h] + k) for k in range(NK)]
+        [
+            Pieces(
+                [(wt_h.at[o, pl.ds(KC * k, KC), pl.ds(256 * h, 256)], wt.at[h, k, o]) for o in range(3)],
+                wt.at[h, k], (4, 30)[h] + k,
+            )
+            for k in range(NK)
+        ]
         for h in range(2)
     ]
     small = [load(a, b, 22 + n) for n, (a, b) in enumerate(zip((g1_h, s1_h, g2_h, s2_h, g3_h, s3_h), (g1, s1, g2, s2, g3, s3)))]
@@ -102,7 +129,7 @@
     def conv_one(k, h):
         empty = jnp.zeros((SPOTS, KC), BF16)
 
-        def rows(p, _):
+        def rows(p, carry):
             taps = []
             for o in range(3):
                 blocks = []
@@ -117,13 +144,20 @@
             w = wt[h, k].reshape(3 * KC, 256)
             r = jnp.dot(lhs, w, preferred_element_type=F32)
             at = pl.ds(pl.multiple_of(p * 512, 512), 512)
+            out = list(carry)
             for c in range(2):
                 q = 2 * h + c
                 v = r[:, 128 * c : 128 * (c + 1)]
-                acc[q, at, :] = v if k == 0 else acc[q, at, :] + v
-            return 0
-
-        lax.fori_loop(0, CLIPS // 4, rows, 0)
+                if k > 0:
+                    v = acc[q, at, :] + v
+                acc[q, at, :] = v
+                if k == NK - 1:
+                    a, b = sums_of(v)
+                    out[2 * c] = out[2 * c] + a
+                    out[2 * c + 1] = out[2 * c + 1] + b
+            return tuple(out)
+
+        return lax.fori_loop(0, CLIPS // 4, rows, zeros[:4])
 
     def q_region(p, phase):
         at = [pl.ds(xyz[a], 1) for a in range(3)]
@@ -210,17 +244,6 @@
     def rows_of(ref, at, chunks=(0, 1, 2, 3)):
         return jnp.concatenate([ref[q, at, :] for q in chunks], axis=1)
 
-    def total_of(ref, chunks=(0, 1, 2, 3)):
-        def body(p, carry):
-            out = list(carry)
-            for n, q in enumerate(chunks):
-                a, b = sums_of(ref[q, pl.ds(pl.multiple_of(p * 128, 128), 128), :])
-                out[2 * n] = out[2 * n] + a
-                out[2 * n + 1] = out[2 * n + 1] + b
-            return tuple(out)
-
-        return lax.fori_loop(0, ROWS // 128, body, zeros[: 2 * len(chunks)])
-
     to_scalar = pltpu.make_async_copy(tabv, tabs, hsem.at[15])
 
     def find_picks():
@@ -232,12 +255,11 @@
             picks[0, k] = (yz - j // 2 + PLANE - 1) % PLANE
             picks[1, k] = jnp.where(j % 2 == core, 1, 0).astype(I32)
 
+    feat_loads[1].start()
+    wt_loads[0][1].start()
     for k in range(NK):
         feat_loads[k].wait()
         wt_loads[0][k].wait()
-        for ahead in {0: (1, 2), 1: (3,)}.get(k, ()):
-            feat_loads[ahead].start()
-            wt_loads[0][ahead].start()
         if k == 0:
             for d in small:
                 d.start()
@@ -250,7 +272,10 @@
             for d in we_loads:
                 d.start()
             wk_load.start()
-        conv_one(k, 0)
+        parts = conv_one(k, 0)
+        if k + 2 < NK:
+            feat_loads[k + 2].start()
+            wt_loads[0][k + 2].start()
         if k == 2:
             pl.semaphore_wait(barrier, CHIPS - 1 + 4)
             for d in small:
@@ -261,11 +286,11 @@
                     device_id=axis_peer(0, n), device_id_type=MESH,
                 ).start()
             q_send(0)
-    put_stats(0, total_of(acc, (0, 1)), (0, 1))
+    put_stats(0, parts, (0, 1))
     plane_send(0)
     for k in range(NK):
         wt_loads[1][k].wait()
-        conv_one(k, 1)
+        parts = conv_one(k, 1)
         if k == 1:
             q_wait(0, 1)
             q_send(1)
@@ -273,7 +298,7 @@
             to_scalar.start()
         if k == 2:
             find_picks()
-    put_stats(6, total_of(acc, (2, 3)), (2, 3))
+    put_stats(6, parts, (2, 3))
     plane_send(6)
 
     zq = jnp.dot(qmine[...], wq[...], preferred_element_type=F32)
@@ -320,7 +345,7 @@
 
         lax.fori_loop(0, CLIPS // 2, norm_one, 0)
 
-    def row_conv(h, r, base, tap, taps):
+    def row_conv(h, r, base, tap, taps, carry):
         lanes = slice(256 * h, 256 * (h + 1))
         lhs = jnp.concatenate(
             [act[base + d, c : c + SIDE, :, lanes].reshape(256, 256) for d in range(taps) for c in range(3)], axis=1
@@ -328,45 +353,49 @@
         w = ws[pl.ds(tap, 3 * taps), lanes].reshape(3 * taps * 256, INNER)
         v = jnp.dot(lhs, w, preferred_element_type=F32)
         at = pl.ds(pl.multiple_of(r * 256, 256), 256)
+        out = list(carry)
         for q in range(4):
             part = v[:, 128 * q : 128 * (q + 1)]
-            second[q, at, :] = part if h == 0 else second[q, at, :] + part
-
-    def edges(h):
-        def edge(n, _):
-            row_conv(h, 3 * n, 2 * n, 3 - 3 * n, 2)
-            return 0
-
-        lax.fori_loop(0, 2, edge, 0)
-
-    def middles(h):
-        def middle(n, _):
-            row_conv(h, 1 + n, n, 0, 3)
-            return 0
-
-        lax.fori_loop(0, 2, middle, 0)
-
-    carry = queue_part(0, 7, carry)
+            if h == 1:
+                part = second[q, at, :] + part
+                a, b = sums_of(part)
+                out[2 * q] = out[2 * q] + a
+                out[2 * q + 1] = out[2 * q + 1] + b
+            second[q, at, :] = part
+        return tuple(out)
+
+    def edges(h, sums):
+        def edge(n, sums):
+            return row_conv(h, 3 * n, 2 * n, 3 - 3 * n, 2, sums)
+
+        return lax.fori_loop(0, 2, edge, sums)
+
+    def middles(h, sums):
+        def middle(n, sums):
+            return row_conv(h, 1 + n, n, 0, 3, sums)
+
+        return lax.fori_loop(0, 2, middle, sums)
+
+    carry = queue_part(0, 5, carry)
     plane_forward(6)
     q_wait(1, 1)
     q_send(2, (1, 2))
     tile = line_finish(0)
     normalize_one(0, tile)
     ws_load.wait()
-    edges(0)
-    middles(0)
+    edges(0, ())
+    middles(0, ())
     tile = line_finish(6)
     q_send(2, (0,))
     q_send(3, (1, 2))
     normalize_one(1, tile)
-    edges(1)
-    middles(1)
-    put_stats(1, total_of(second))
+    sums = middles(1, edges(1, zeros))
+    put_stats(1, sums)
     plane_send(1)
     q_send(3, (0,))
-    carry = queue_part(7, 15, carry)
+    carry = queue_part(5, 13, carry)
     plane_forward(1)
-    carry = queue_part(15, 16, carry)
+    carry = queue_part(13, 16, carry)
     tile = line_finish(1)
     q_wait(2, 1)
     q_wait(3, 1)
@@ -443,7 +472,7 @@
     grad = (mix / whole + (e_pos / whole - 1.0) * held) * 5.0
     radial = jnp.sum(unit * grad, axis=-1, keepdims=True)
     gvec[...] = ((grad - radial * unit) / length).astype(BF16)
-    for k in range(1, CHIPS):
+    for k in sorted(range(1, CHIPS), key=hops, reverse=True):
         pltpu.make_async_remote_copy(
             src_ref=gvec, dst_ref=gall.at[chip], send_sem=gsem.at[0], recv_sem=gsem.at[1],
             device_id=chip_peer(k), device_id_type=MESH,

time: 65.7 us -> 64.4 us (0.980)
  Pallas kernels: 64.9 us -> 63.6 us
    pallas_call x1, Pallas kernels: 60.7 us -> 59.3 us  [local(): pl.pallas_call(kernel, name='moco', out_shape=(jax.ShapeDtypeStruct((CLIP...]
where the time goes in v6:
time: 64.4 us; the launch traced here: 64.2 us
  Pallas kernels  63.6 us (99%)
    pallas_call x1, Pallas kernels, local(): pl.pallas_call(kernel, name='moco', out_shape=(jax.ShapeDtypeStruct((CLIP...  59.3 us
    pallas_call x1, Pallas kernels, local(): pl.pallas_call(last, name='last', out_shape=(jax.ShapeDtypeStruct((CLIPS,...  4.24 us

profile of v6, /device:TPU:1, one launch (start us, length us, event | category | flops | bytes accessed | tf_op | source)
XLA Modules:
  0.0 64.2 jit_solution(7989872853707977184)
XLA Ops:
  0.6 59.3 %moco.1 = (bf16[8,128]{1,0:T(8,128)(2,1)}, bf16[2048,1024]{1,0:T(8,128)(2,1)}, bf16[2,64,8,128]{3,2,1,0:T(8,128)(2,1)}) custom-call(s32[8]{0:T(128)} %starts_h.1, bf16[8,12,16,2048]{3,2,1,0:T(8,128)(2,1)} %feats.1, s32[1,32]{1,0:T(1,128)} %shuf_h.1, bf16[8,2048]{1,0:T(8,128)(2,1)} %qf_h.1, bf16[3,2048,512]{2,1,0:T(8,128)(2,1)} %wt_h.1, ...), custom_call_target="tpu_custom_call" | custom-call | tf_op jit(solution)/shard_map/moco/pallas_call | solution.py:553
  60.0 4.2 %last.1 = (bf16[8,128]{1,0:T(8,128)(2,1)}, f32[2048,128]{1,0:T(8,128)}) custom-call(bf16[8,128]{1,0:T(8,128)(2,1)} %get-tuple-element.5.keys_ref, bf16[2048,1024]{1,0:T(8,128)(2,1)} %get-tuple-element.6.q_ref, bf16[1024,128]{1,0:T(8,128)(2,1)} %bitcast.7), custom_call_target="tpu_custom_call" | custom-call | tf_op jit(solution)/shard_map/last/pallas_call | solution.py:608

commit v7 on v6

--- a/solution.py
+++ b/solution.py
@@ -143,7 +143,7 @@
             lhs = jnp.concatenate(taps, axis=1)
             w = wt[h, k].reshape(3 * KC, 256)
             r = jnp.dot(lhs, w, preferred_element_type=F32)
-            at = pl.ds(pl.multiple_of(p * 512, 512), 512)
+            at = pl.ds(p * 512, 512)
             out = list(carry)
             for c in range(2):
                 q = 2 * h + c
@@ -157,7 +157,7 @@
                     out[2 * c + 1] = out[2 * c + 1] + b
             return tuple(out)
 
-        return lax.fori_loop(0, CLIPS // 4, rows, zeros[:4])
+        return rows(1, rows(0, zeros[:4]))
 
     def q_region(p, phase):
         at = [pl.ds(xyz[a], 1) for a in range(3)]
@@ -291,12 +291,12 @@
     for k in range(NK):
         wt_loads[1][k].wait()
         parts = conv_one(k, 1)
-        if k == 1:
+        if k == 2:
             q_wait(0, 1)
             q_send(1)
             await_bytes(tabv.at[pl.ds(0, 3)], tsem.at[1])
             to_scalar.start()
-        if k == 2:
+        if k == 3:
             find_picks()
     put_stats(6, parts, (2, 3))
     plane_send(6)
@@ -352,7 +352,7 @@
         )
         w = ws[pl.ds(tap, 3 * taps), lanes].reshape(3 * taps * 256, INNER)
         v = jnp.dot(lhs, w, preferred_element_type=F32)
-        at = pl.ds(pl.multiple_of(r * 256, 256), 256)
+        at = pl.ds(r * 256, 256)
         out = list(carry)
         for q in range(4):
             part = v[:, 128 * q : 128 * (q + 1)]
@@ -368,13 +368,13 @@
         def edge(n, sums):
             return row_conv(h, 3 * n, 2 * n, 3 - 3 * n, 2, sums)
 
-        return lax.fori_loop(0, 2, edge, sums)
+        return edge(1, edge(0, sums))
 
     def middles(h, sums):
         def middle(n, sums):
             return row_conv(h, 1 + n, n, 0, 3, sums)
 
-        return lax.fori_loop(0, 2, middle, sums)
+        return middle(1, middle(0, sums))
 
     carry = queue_part(0, 5, carry)
     plane_forward(6)
@@ -443,19 +443,20 @@
         cols = slice(INNER * q, INNER * (q + 1))
         scale, shift = affine(line_finish(2 + q), g3[:, cols], s3[:, cols])
 
-        def pool(n, _):
-            at = pl.ds(pl.multiple_of(n * 128, 128), 128)
-            first = starts[n]
-            for c in range(4):
-                lanes = slice(128 * c, 128 * (c + 1))
-                kept = jnp.concatenate([xall[q][n, first + t, :, lanes] for t in range(FRAMES)], axis=0).astype(F32)
-                v = jnp.maximum(third[q, at, lanes] * scale[:, lanes] + shift[:, lanes] + kept, 0.0)
-                pooled[n, :, INNER * q + 128 * c : INNER * q + 128 * (c + 1)] = jnp.sum(
-                    v.reshape(16, 8, 128), axis=0
-                )
+        def pool(pair, _):
+            for n in (2 * pair, 2 * pair + 1):
+                at = pl.ds(pl.multiple_of(n * 128, 128), 128)
+                first = starts[n]
+                for c in range(4):
+                    lanes = slice(128 * c, 128 * (c + 1))
+                    kept = jnp.concatenate([xall[q][n, first + t, :, lanes] for t in range(FRAMES)], axis=0).astype(F32)
+                    v = jnp.maximum(third[q, at, lanes] * scale[:, lanes] + shift[:, lanes] + kept, 0.0)
+                    pooled[n, :, INNER * q + 128 * c : INNER * q + 128 * (c + 1)] = jnp.sum(
+                        v.reshape(16, 8, 128), axis=0
+                    )
             return 0
 
-        lax.fori_loop(0, CLIPS, pool, 0)
+        lax.fori_loop(0, CLIPS // 2, pool, 0)
     wk_load.wait()
     mean = jnp.sum(pooled[...], axis=1) * (1.0 / 128.0)
     projected = jnp.dot(mean.astype(BF16), wk[...], preferred_element_type=F32)

time: 64.4 us -> 63.2 us (0.981)
  Pallas kernels: 63.6 us -> 62.2 us
    pallas_call x1, Pallas kernels: 59.3 us -> 58 us  [local(): pl.pallas_call(kernel, name='moco', out_shape=(jax.ShapeDtypeStruct((CLIP...]
where the time goes in v7:
time: 63.2 us; the launch traced here: 63 us
  Pallas kernels  62.2 us (98%)
  between operations  0.81 us (1%)
    pallas_call x1, Pallas kernels, local(): pl.pallas_call(kernel, name='moco', out_shape=(jax.ShapeDtypeStruct((CLIP...  58 us
    pallas_call x1, Pallas kernels, local(): pl.pallas_call(last, name='last', out_shape=(jax.ShapeDtypeStruct((CLIPS,...  4.23 us

profile of v7, /device:TPU:1, one launch (start us, length us, event | category | flops | bytes accessed | tf_op | source)
XLA Modules:
  0.0 63.0 jit_solution(14594226111073382468)
XLA Ops:
  0.6 58.0 %moco.1 = (bf16[8,128]{1,0:T(8,128)(2,1)}, bf16[2048,1024]{1,0:T(8,128)(2,1)}, bf16[2,64,8,128]{3,2,1,0:T(8,128)(2,1)}) custom-call(s32[8]{0:T(128)} %starts_h.1, bf16[8,12,16,2048]{3,2,1,0:T(8,128)(2,1)} %feats.1, s32[1,32]{1,0:T(1,128)} %shuf_h.1, bf16[8,2048]{1,0:T(8,128)(2,1)} %qf_h.1, bf16[3,2048,512]{2,1,0:T(8,128)(2,1)} %wt_h.1, ...), custom_call_target="tpu_custom_call" | custom-call | tf_op jit(solution)/shard_map/moco/pallas_call | solution.py:554
  58.6 4.2 %last.1 = (bf16[8,128]{1,0:T(8,128)(2,1)}, f32[2048,128]{1,0:T(8,128)}) custom-call(bf16[8,128]{1,0:T(8,128)(2,1)} %get-tuple-element.5.keys_ref, bf16[2048,1024]{1,0:T(8,128)(2,1)} %get-tuple-element.6.q_ref, bf16[1024,128]{1,0:T(8,128)(2,1)} %bitcast.7), custom_call_target="tpu_custom_call" | custom-call | tf_op jit(solution)/shard_map/last/pallas_call | solution.py:609
